TPU v7x, 128 devices: a whole 4x4x4 slice. The times are simulated.
128 devices in a mesh: row: 8 (over y_hi, z), col: 16 (over y_lo, x, core).
Axes of the slice: x: 4, y: 4 (y_hi: 2, y_lo: 2; y = y_hi * 2 + y_lo), z: 4, core: 2. Of those that a mesh axis runs over, the one named last changes fastest.
Arguments:
- a_tiles: float32 [8, 16, 8, 128, 128], P('row', 'col'), may hold values from -6 to 6
- b_tiles: float32 [8, 16, 8, 128, 128], P('row', 'col'), may hold values from -0.25 to 0.25
- pair_lists: int32 [8, 16, 16, 3, 32], P('row', 'col'), may hold values from 0 to 63, as said below
- stack_counts: int32 [8, 16, 16], P('row', 'col'), may hold values from 1 to 32, as said below
Outputs:
- c_tiles: float32 [8, 16, 32, 128, 128], P('row', 'col')
Inputs may be any that keep to these rules, and one draw needn't show every extreme that they name: `pair_lists`: entry 0 of a list column is an A tile slot below 8, entry 1 a tile of bcol below 64, entry 2 a product tile below 32; entries past the live count are valid indices that do not count. `stack_counts`: live entries of each list; in every draw some list has all 32 live.
All inputs are finite; a program needn't handle non-finite values.
Results may differ from a plain program's by a relative error of at most 0.0003.
Values sent between devices are 32-bit elements; how exact they have to be, the bound alone decides.
No kernel may reach another device: no remote copies, remote signals or barrier semaphores. Data moves between devices by JAX's collectives and lax.ppermute only.
A program may use at most 64 MiB of HBM per device.

v0:
```python
import math

import jax
import jax.numpy as jnp
from jax import lax
from jax.sharding import PartitionSpec as P

CT = 32


def shifted(value, axis, steps):
    count = lax.axis_size(axis)
    pairs = [(source, (source + steps) % count) for source in range(count)]
    return lax.ppermute(value, axis, pairs)


def add_block(totals, a_panel, b_all, stack_list, count_live, group_size):
    is_live = jnp.arange(group_size, dtype=jnp.int32) < count_live
    a_pick = (
        stack_list[0][:, None] == jnp.arange(a_panel.shape[0], dtype=jnp.int32)[None, :]
    ).astype(jnp.float32)
    b_pick = (
        stack_list[1][:, None] == jnp.arange(b_all.shape[0], dtype=jnp.int32)[None, :]
    ).astype(jnp.float32)
    c_place = (
        jnp.arange(totals.shape[0], dtype=jnp.int32)[:, None] == stack_list[2][None, :]
    ) & is_live[None, :]
    c_place = c_place.astype(jnp.float32)
    left_tiles = jnp.einsum(
        "gs,sij->gij",
        a_pick,
        a_panel,
        precision=lax.Precision.HIGHEST,
        preferred_element_type=jnp.float32,
    )
    right_tiles = jnp.einsum(
        "gs,sij->gij",
        b_pick,
        b_all,
        precision=lax.Precision.HIGHEST,
        preferred_element_type=jnp.float32,
    )
    products = jnp.einsum(
        "gij,gjk->gik",
        left_tiles,
        right_tiles,
        precision=lax.Precision.HIGHEST,
        preferred_element_type=jnp.float32,
    )
    return totals + jnp.einsum(
        "mg,gik->mik",
        c_place,
        products,
        precision=lax.Precision.HIGHEST,
        preferred_element_type=jnp.float32,
    )


def apply_panel(totals, a_panel, b_all, stack_list, count_live):
    entries = stack_list.shape[1]
    group_size = math.gcd(entries, 32)
    totals = add_block(totals, a_panel, b_all, stack_list, count_live, group_size)
    return totals


def body(a_tiles, b_tiles, pair_lists, stack_counts):
    tile_width = a_tiles.shape[3]
    col_count = lax.axis_size("col")
    own_column = lax.axis_index("col")
    gathered_b = lax.all_gather(b_tiles, "row", axis=0, tiled=True)
    b_all = gathered_b.reshape(-1, tile_width, tile_width)
    lists_all = pair_lists[0, 0]
    counts_all = stack_counts[0, 0]

    def visit(totals, a_panel, panel_index, keep_flag):
        stack_list = lax.dynamic_index_in_dim(lists_all, panel_index, 0, keepdims=False)
        count_live = (
            lax.dynamic_index_in_dim(counts_all, panel_index, 0, keepdims=False) * keep_flag
        )
        return apply_panel(totals, a_panel, b_all, stack_list, count_live)

    totals = jnp.zeros((CT, tile_width, tile_width), jnp.float32)
    own_panel = a_tiles[0, 0]
    totals = visit(totals, own_panel, own_column, 1)

    def next_stop(stop_index, loop_state):
        totals_in, moving = loop_state
        moving = shifted(moving, "col", 1)
        panel_index = (own_column - stop_index) % col_count
        return (visit(totals_in, moving, panel_index, 1), moving)

    totals, moving = lax.fori_loop(1, col_count, next_stop, (totals, own_panel))
    return totals[None, None]


def solution(mesh):
    return jax.shard_map(
        body,
        mesh=mesh,
        in_specs=(
            P("row", "col", None, None, None),
            P("row", "col", None, None, None),
            P("row", "col", None, None, None),
            P("row", "col", None),
        ),
        out_specs=P("row", "col", None, None, None),
        check_vma=False,
    )
```

profile of v0, /device:TPU:0, one launch (start us, length us, event | category | flops | bytes accessed | tf_op | source)
XLA Modules:
  0.0 401.2 jit_solution(11839348177748028509)
XLA Ops:
  12.1 71.7 %all-gather.2.cloned.1.call-done = f32[8,1,8,128,128]{4,3,2,1,0:T(8,128)} async-done(((f32[1,1,8,128,128]{4,3,2,1,0:T(8,128)}), f32[8,1,8,128,128]{4,3,2,1,0:T(8,128)}) %all-gather.2.cloned.1.call-update) | async-done | bytes 4194320 | tf_op jit(solution)/shard_map/all_gather | solution.py:70
  83.8 6.1 %fusion.23 = f32[32,128,128]{2,0,1:T(8,128)S(1)} fusion(f32[64,128,128]{2,1,0:T(8,128)} %bitcast.51, s32[32]{0:T(128)S(1)} %get-tuple-element.202), kind=kOutput, calls=%fused_computation.26 | convolution fusion | flops 402655232 | bytes 6291584 | tf_op jit(solution)/shard_map/gs,sij->gij/dot_general | solution.py:36
  89.9 4.6 %fusion.27 = f32[32,128,128]{2,1,0:T(8,128)S(1)} fusion(f32[32,128,128]{2,0,1:T(8,128)S(1)} %fusion.23, f32[32,128,128]{2,0,1:T(8,128)S(1)} %fusion.30), kind=kOutput, calls=%fused_computation.30 | convolution fusion | flops 805306368 | bytes 6291456 | tf_op jit(solution)/shard_map/gij,gjk->gik/dot_general | solution.py:43
  96.9 294.9 %while.17 = (s32[]{:T(128)}, f32[32,128,128]{2,0,1:T(8,128)S(1)}, f32[8,128,128]{2,1,0:T(8,128)S(1)}, s32[]{:T(128)}, s32[16,3,32]{2,1,0:T(4,128)S(1)}, /*index=...) while((s32[]{:T(128)}, f32[32,128,128]{2,0,1:T(8,128)S(1)}, ...), condition=%wide.region_1.2_spmd, body=%wide.region_0.1_spmd.sunk | while | flops 1460146432 | bytes 24643844 | solution.py:92
  98.4 6.1 %fusion.66 = f32[32,128,128]{2,0,1:T(8,128)S(1)} fusion(f32[64,128,128]{2,1,0:T(8,128)} %get-tuple-element.280, s32[32]{0:T(128)S(1)} %get-tuple-element.249), kind=kOutput, calls=%fused_computation.clone.1 | convolution fusion | flops 402655232 | bytes 6291584 | tf_op jit(solution)/shard_map/while/body/eval_jaxpr/gs,sij->gij/dot_general | solution.py:36
  104.5 3.4 collective-permute-done
  108.9 4.6 %fusion.68 = f32[32,128,128]{2,1,0:T(8,128)S(1)} fusion(f32[32,128,128]{2,0,1:T(8,128)S(1)} %fusion.66, f32[32,128,128]{2,0,1:T(8,128)S(1)} %fusion.67), kind=kOutput, calls=%fused_computation.4.clone.1 | convolution fusion | flops 805306368 | bytes 6291456 | tf_op jit(solution)/shard_map/while/body/eval_jaxpr/gij,gjk->gik/dot_general | solution.py:43
  113.5 3.1 fusion.69
  118.1 6.1 %fusion.66 = f32[32,128,128]{2,0,1:T(8,128)S(1)} fusion(f32[64,128,128]{2,1,0:T(8,128)} %get-tuple-element.280, s32[32]{0:T(128)S(1)} %get-tuple-element.249), kind=kOutput, calls=%fused_computation.clone.1 | convolution fusion | flops 402655232 | bytes 6291584 | tf_op jit(solution)/shard_map/while/body/eval_jaxpr/gs,sij->gij/dot_general | solution.py:36
  124.2 3.4 collective-permute-done
  128.6 4.6 %fusion.68 = f32[32,128,128]{2,1,0:T(8,128)S(1)} fusion(f32[32,128,128]{2,0,1:T(8,128)S(1)} %fusion.66, f32[32,128,128]{2,0,1:T(8,128)S(1)} %fusion.67), kind=kOutput, calls=%fused_computation.4.clone.1 | convolution fusion | flops 805306368 | bytes 6291456 | tf_op jit(solution)/shard_map/while/body/eval_jaxpr/gij,gjk->gik/dot_general | solution.py:43
  133.2 3.1 fusion.69
  137.7 6.1 %fusion.66 = f32[32,128,128]{2,0,1:T(8,128)S(1)} fusion(f32[64,128,128]{2,1,0:T(8,128)} %get-tuple-element.280, s32[32]{0:T(128)S(1)} %get-tuple-element.249), kind=kOutput, calls=%fused_computation.clone.1 | convolution fusion | flops 402655232 | bytes 6291584 | tf_op jit(solution)/shard_map/while/body/eval_jaxpr/gs,sij->gij/dot_general | solution.py:36
  143.8 3.4 collective-permute-done
  148.2 4.6 %fusion.68 = f32[32,128,128]{2,1,0:T(8,128)S(1)} fusion(f32[32,128,128]{2,0,1:T(8,128)S(1)} %fusion.66, f32[32,128,128]{2,0,1:T(8,128)S(1)} %fusion.67), kind=kOutput, calls=%fused_computation.4.clone.1 | convolution fusion | flops 805306368 | bytes 6291456 | tf_op jit(solution)/shard_map/while/body/eval_jaxpr/gij,gjk->gik/dot_general | solution.py:43
  152.8 3.1 fusion.69
  157.4 6.1 %fusion.66 = f32[32,128,128]{2,0,1:T(8,128)S(1)} fusion(f32[64,128,128]{2,1,0:T(8,128)} %get-tuple-element.280, s32[32]{0:T(128)S(1)} %get-tuple-element.249), kind=kOutput, calls=%fused_computation.clone.1 | convolution fusion | flops 402655232 | bytes 6291584 | tf_op jit(solution)/shard_map/while/body/eval_jaxpr/gs,sij->gij/dot_general | solution.py:36
  163.5 3.4 collective-permute-done
  167.9 4.6 %fusion.68 = f32[32,128,128]{2,1,0:T(8,128)S(1)} fusion(f32[32,128,128]{2,0,1:T(8,128)S(1)} %fusion.66, f32[32,128,128]{2,0,1:T(8,128)S(1)} %fusion.67), kind=kOutput, calls=%fused_computation.4.clone.1 | convolution fusion | flops 805306368 | bytes 6291456 | tf_op jit(solution)/shard_map/while/body/eval_jaxpr/gij,gjk->gik/dot_general | solution.py:43
  172.5 3.1 fusion.69
  177.0 6.1 %fusion.66 = f32[32,128,128]{2,0,1:T(8,128)S(1)} fusion(f32[64,128,128]{2,1,0:T(8,128)} %get-tuple-element.280, s32[32]{0:T(128)S(1)} %get-tuple-element.249), kind=kOutput, calls=%fused_computation.clone.1 | convolution fusion | flops 402655232 | bytes 6291584 | tf_op jit(solution)/shard_map/while/body/eval_jaxpr/gs,sij->gij/dot_general | solution.py:36
  183.1 3.4 collective-permute-done
  187.5 4.6 %fusion.68 = f32[32,128,128]{2,1,0:T(8,128)S(1)} fusion(f32[32,128,128]{2,0,1:T(8,128)S(1)} %fusion.66, f32[32,128,128]{2,0,1:T(8,128)S(1)} %fusion.67), kind=kOutput, calls=%fused_computation.4.clone.1 | convolution fusion | flops 805306368 | bytes 6291456 | tf_op jit(solution)/shard_map/while/body/eval_jaxpr/gij,gjk->gik/dot_general | solution.py:43
  192.1 3.1 fusion.69
  196.7 6.1 %fusion.66 = f32[32,128,128]{2,0,1:T(8,128)S(1)} fusion(f32[64,128,128]{2,1,0:T(8,128)} %get-tuple-element.280, s32[32]{0:T(128)S(1)} %get-tuple-element.249), kind=kOutput, calls=%fused_computation.clone.1 | convolution fusion | flops 402655232 | bytes 6291584 | tf_op jit(solution)/shard_map/while/body/eval_jaxpr/gs,sij->gij/dot_general | solution.py:36
  202.7 3.4 collective-permute-done
  207.2 4.6 %fusion.68 = f32[32,128,128]{2,1,0:T(8,128)S(1)} fusion(f32[32,128,128]{2,0,1:T(8,128)S(1)} %fusion.66, f32[32,128,128]{2,0,1:T(8,128)S(1)} %fusion.67), kind=kOutput, calls=%fused_computation.4.clone.1 | convolution fusion | flops 805306368 | bytes 6291456 | tf_op jit(solution)/shard_map/while/body/eval_jaxpr/gij,gjk->gik/dot_general | solution.py:43
  211.8 3.1 fusion.69
  216.3 6.1 %fusion.66 = f32[32,128,128]{2,0,1:T(8,128)S(1)} fusion(f32[64,128,128]{2,1,0:T(8,128)} %get-tuple-element.280, s32[32]{0:T(128)S(1)} %get-tuple-element.249), kind=kOutput, calls=%fused_computation.clone.1 | convolution fusion | flops 402655232 | bytes 6291584 | tf_op jit(solution)/shard_map/while/body/eval_jaxpr/gs,sij->gij/dot_general | solution.py:36
  222.4 3.4 collective-permute-done
  226.8 4.6 %fusion.68 = f32[32,128,128]{2,1,0:T(8,128)S(1)} fusion(f32[32,128,128]{2,0,1:T(8,128)S(1)} %fusion.66, f32[32,128,128]{2,0,1:T(8,128)S(1)} %fusion.67), kind=kOutput, calls=%fused_computation.4.clone.1 | convolution fusion | flops 805306368 | bytes 6291456 | tf_op jit(solution)/shard_map/while/body/eval_jaxpr/gij,gjk->gik/dot_general | solution.py:43
  231.4 3.1 fusion.69
  236.0 6.1 %fusion.66 = f32[32,128,128]{2,0,1:T(8,128)S(1)} fusion(f32[64,128,128]{2,1,0:T(8,128)} %get-tuple-element.280, s32[32]{0:T(128)S(1)} %get-tuple-element.249), kind=kOutput, calls=%fused_computation.clone.1 | convolution fusion | flops 402655232 | bytes 6291584 | tf_op jit(solution)/shard_map/while/body/eval_jaxpr/gs,sij->gij/dot_general | solution.py:36
  242.0 3.4 collective-permute-done
  246.5 4.6 %fusion.68 = f32[32,128,128]{2,1,0:T(8,128)S(1)} fusion(f32[32,128,128]{2,0,1:T(8,128)S(1)} %fusion.66, f32[32,128,128]{2,0,1:T(8,128)S(1)} %fusion.67), kind=kOutput, calls=%fused_computation.4.clone.1 | convolution fusion | flops 805306368 | bytes 6291456 | tf_op jit(solution)/shard_map/while/body/eval_jaxpr/gij,gjk->gik/dot_general | solution.py:43
  251.1 3.1 fusion.69
  255.6 6.1 %fusion.66 = f32[32,128,128]{2,0,1:T(8,128)S(1)} fusion(f32[64,128,128]{2,1,0:T(8,128)} %get-tuple-element.280, s32[32]{0:T(128)S(1)} %get-tuple-element.249), kind=kOutput, calls=%fused_computation.clone.1 | convolution fusion | flops 402655232 | bytes 6291584 | tf_op jit(solution)/shard_map/while/body/eval_jaxpr/gs,sij->gij/dot_general | solution.py:36
  261.7 3.4 collective-permute-done
  266.1 4.6 %fusion.68 = f32[32,128,128]{2,1,0:T(8,128)S(1)} fusion(f32[32,128,128]{2,0,1:T(8,128)S(1)} %fusion.66, f32[32,128,128]{2,0,1:T(8,128)S(1)} %fusion.67), kind=kOutput, calls=%fused_computation.4.clone.1 | convolution fusion | flops 805306368 | bytes 6291456 | tf_op jit(solution)/shard_map/while/body/eval_jaxpr/gij,gjk->gik/dot_general | solution.py:43
  270.7 3.1 fusion.69
  275.3 6.1 %fusion.66 = f32[32,128,128]{2,0,1:T(8,128)S(1)} fusion(f32[64,128,128]{2,1,0:T(8,128)} %get-tuple-element.280, s32[32]{0:T(128)S(1)} %get-tuple-element.249), kind=kOutput, calls=%fused_computation.clone.1 | convolution fusion | flops 402655232 | bytes 6291584 | tf_op jit(solution)/shard_map/while/body/eval_jaxpr/gs,sij->gij/dot_general | solution.py:36
  281.3 3.4 collective-permute-done
  285.8 4.6 %fusion.68 = f32[32,128,128]{2,1,0:T(8,128)S(1)} fusion(f32[32,128,128]{2,0,1:T(8,128)S(1)} %fusion.66, f32[32,128,128]{2,0,1:T(8,128)S(1)} %fusion.67), kind=kOutput, calls=%fused_computation.4.clone.1 | convolution fusion | flops 805306368 | bytes 6291456 | tf_op jit(solution)/shard_map/while/body/eval_jaxpr/gij,gjk->gik/dot_general | solution.py:43
  290.3 3.1 fusion.69
  294.9 6.1 %fusion.66 = f32[32,128,128]{2,0,1:T(8,128)S(1)} fusion(f32[64,128,128]{2,1,0:T(8,128)} %get-tuple-element.280, s32[32]{0:T(128)S(1)} %get-tuple-element.249), kind=kOutput, calls=%fused_computation.clone.1 | convolution fusion | flops 402655232 | bytes 6291584 | tf_op jit(solution)/shard_map/while/body/eval_jaxpr/gs,sij->gij/dot_general | solution.py:36
  301.0 3.4 collective-permute-done
  305.4 4.6 %fusion.68 = f32[32,128,128]{2,1,0:T(8,128)S(1)} fusion(f32[32,128,128]{2,0,1:T(8,128)S(1)} %fusion.66, f32[32,128,128]{2,0,1:T(8,128)S(1)} %fusion.67), kind=kOutput, calls=%fused_computation.4.clone.1 | convolution fusion | flops 805306368 | bytes 6291456 | tf_op jit(solution)/shard_map/while/body/eval_jaxpr/gij,gjk->gik/dot_general | solution.py:43
  310.0 3.1 fusion.69
  314.6 6.1 %fusion.66 = f32[32,128,128]{2,0,1:T(8,128)S(1)} fusion(f32[64,128,128]{2,1,0:T(8,128)} %get-tuple-element.280, s32[32]{0:T(128)S(1)} %get-tuple-element.249), kind=kOutput, calls=%fused_computation.clone.1 | convolution fusion | flops 402655232 | bytes 6291584 | tf_op jit(solution)/shard_map/while/body/eval_jaxpr/gs,sij->gij/dot_general | solution.py:36
  320.6 3.4 collective-permute-done
  325.1 4.6 %fusion.68 = f32[32,128,128]{2,1,0:T(8,128)S(1)} fusion(f32[32,128,128]{2,0,1:T(8,128)S(1)} %fusion.66, f32[32,128,128]{2,0,1:T(8,128)S(1)} %fusion.67), kind=kOutput, calls=%fused_computation.4.clone.1 | convolution fusion | flops 805306368 | bytes 6291456 | tf_op jit(solution)/shard_map/while/body/eval_jaxpr/gij,gjk->gik/dot_general | solution.py:43
  329.6 3.1 fusion.69
  334.2 6.1 %fusion.66 = f32[32,128,128]{2,0,1:T(8,128)S(1)} fusion(f32[64,128,128]{2,1,0:T(8,128)} %get-tuple-element.280, s32[32]{0:T(128)S(1)} %get-tuple-element.249), kind=kOutput, calls=%fused_computation.clone.1 | convolution fusion | flops 402655232 | bytes 6291584 | tf_op jit(solution)/shard_map/while/body/eval_jaxpr/gs,sij->gij/dot_general | solution.py:36
  340.3 3.4 collective-permute-done
  344.7 4.6 %fusion.68 = f32[32,128,128]{2,1,0:T(8,128)S(1)} fusion(f32[32,128,128]{2,0,1:T(8,128)S(1)} %fusion.66, f32[32,128,128]{2,0,1:T(8,128)S(1)} %fusion.67), kind=kOutput, calls=%fused_computation.4.clone.1 | convolution fusion | flops 805306368 | bytes 6291456 | tf_op jit(solution)/shard_map/while/body/eval_jaxpr/gij,gjk->gik/dot_general | solution.py:43
  349.3 3.1 fusion.69
  353.8 6.1 %fusion.66 = f32[32,128,128]{2,0,1:T(8,128)S(1)} fusion(f32[64,128,128]{2,1,0:T(8,128)} %get-tuple-element.280, s32[32]{0:T(128)S(1)} %get-tuple-element.249), kind=kOutput, calls=%fused_computation.clone.1 | convolution fusion | flops 402655232 | bytes 6291584 | tf_op jit(solution)/shard_map/while/body/eval_jaxpr/gs,sij->gij/dot_general | solution.py:36
  359.9 3.4 collective-permute-done
  364.4 4.6 %fusion.68 = f32[32,128,128]{2,1,0:T(8,128)S(1)} fusion(f32[32,128,128]{2,0,1:T(8,128)S(1)} %fusion.66, f32[32,128,128]{2,0,1:T(8,128)S(1)} %fusion.67), kind=kOutput, calls=%fused_computation.4.clone.1 | convolution fusion | flops 805306368 | bytes 6291456 | tf_op jit(solution)/shard_map/while/body/eval_jaxpr/gij,gjk->gik/dot_general | solution.py:43
  368.9 3.1 fusion.69
  373.5 6.1 %fusion.66 = f32[32,128,128]{2,0,1:T(8,128)S(1)} fusion(f32[64,128,128]{2,1,0:T(8,128)} %get-tuple-element.280, s32[32]{0:T(128)S(1)} %get-tuple-element.249), kind=kOutput, calls=%fused_computation.clone.1 | convolution fusion | flops 402655232 | bytes 6291584 | tf_op jit(solution)/shard_map/while/body/eval_jaxpr/gs,sij->gij/dot_general | solution.py:36
  379.6 3.4 collective-permute-done
  384.0 4.6 %fusion.68 = f32[32,128,128]{2,1,0:T(8,128)S(1)} fusion(f32[32,128,128]{2,0,1:T(8,128)S(1)} %fusion.66, f32[32,128,128]{2,0,1:T(8,128)S(1)} %fusion.67), kind=kOutput, calls=%fused_computation.4.clone.1 | convolution fusion | flops 805306368 | bytes 6291456 | tf_op jit(solution)/shard_map/while/body/eval_jaxpr/gij,gjk->gik/dot_general | solution.py:43
  388.6 3.1 fusion.69
  (117 shorter events, 46.8 us)
Async XLA Ops:
  6.5 77.3 %all-gather.2.cloned.1.call-start = ((), (), s32[]{:S(2)}) async-start(), calls=%async_computation | async-start | bytes 4718592 | tf_op jit(solution)/shard_map/all_gather | solution.py:70
  94.4 2.4 copy-start
  97.1 10.8 %collective-permute-start = (f32[8,128,128]{2,1,0:T(8,128)S(1)}, f32[8,128,128]{2,1,0:T(8,128)S(1)}, u32[]{:S(2)}, u32[]{:S(2)}) collective-permute-start(f32[8,128,128]{2,1,0:T(8,128)S(1)} %get-tuple-element.265), channel_id=1, source_target_pairs={{0,1},{1,2},{2,3},{3,4},{4,5},{5,6},{6,7},{7,8},{8,9},{9,10},{10,1... | collective-permute-start | bytes 1572872 | tf_op jit(solution)/shard_map/while/body/eval_jaxpr/ppermute | solution.py:14
  116.7 10.8 %collective-permute-start = (f32[8,128,128]{2,1,0:T(8,128)S(1)}, f32[8,128,128]{2,1,0:T(8,128)S(1)}, u32[]{:S(2)}, u32[]{:S(2)}) collective-permute-start(f32[8,128,128]{2,1,0:T(8,128)S(1)} %get-tuple-element.265), channel_id=1, source_target_pairs={{0,1},{1,2},{2,3},{3,4},{4,5},{5,6},{6,7},{7,8},{8,9},{9,10},{10,1... | collective-permute-start | bytes 1572872 | tf_op jit(solution)/shard_map/while/body/eval_jaxpr/ppermute | solution.py:14
  136.4 10.8 %collective-permute-start = (f32[8,128,128]{2,1,0:T(8,128)S(1)}, f32[8,128,128]{2,1,0:T(8,128)S(1)}, u32[]{:S(2)}, u32[]{:S(2)}) collective-permute-start(f32[8,128,128]{2,1,0:T(8,128)S(1)} %get-tuple-element.265), channel_id=1, source_target_pairs={{0,1},{1,2},{2,3},{3,4},{4,5},{5,6},{6,7},{7,8},{8,9},{9,10},{10,1... | collective-permute-start | bytes 1572872 | tf_op jit(solution)/shard_map/while/body/eval_jaxpr/ppermute | solution.py:14
  156.0 10.8 %collective-permute-start = (f32[8,128,128]{2,1,0:T(8,128)S(1)}, f32[8,128,128]{2,1,0:T(8,128)S(1)}, u32[]{:S(2)}, u32[]{:S(2)}) collective-permute-start(f32[8,128,128]{2,1,0:T(8,128)S(1)} %get-tuple-element.265), channel_id=1, source_target_pairs={{0,1},{1,2},{2,3},{3,4},{4,5},{5,6},{6,7},{7,8},{8,9},{9,10},{10,1... | collective-permute-start | bytes 1572872 | tf_op jit(solution)/shard_map/while/body/eval_jaxpr/ppermute | solution.py:14
  175.7 10.8 %collective-permute-start = (f32[8,128,128]{2,1,0:T(8,128)S(1)}, f32[8,128,128]{2,1,0:T(8,128)S(1)}, u32[]{:S(2)}, u32[]{:S(2)}) collective-permute-start(f32[8,128,128]{2,1,0:T(8,128)S(1)} %get-tuple-element.265), channel_id=1, source_target_pairs={{0,1},{1,2},{2,3},{3,4},{4,5},{5,6},{6,7},{7,8},{8,9},{9,10},{10,1... | collective-permute-start | bytes 1572872 | tf_op jit(solution)/shard_map/while/body/eval_jaxpr/ppermute | solution.py:14
  195.3 10.8 %collective-permute-start = (f32[8,128,128]{2,1,0:T(8,128)S(1)}, f32[8,128,128]{2,1,0:T(8,128)S(1)}, u32[]{:S(2)}, u32[]{:S(2)}) collective-permute-start(f32[8,128,128]{2,1,0:T(8,128)S(1)} %get-tuple-element.265), channel_id=1, source_target_pairs={{0,1},{1,2},{2,3},{3,4},{4,5},{5,6},{6,7},{7,8},{8,9},{9,10},{10,1... | collective-permute-start | bytes 1572872 | tf_op jit(solution)/shard_map/while/body/eval_jaxpr/ppermute | solution.py:14
  215.0 10.8 %collective-permute-start = (f32[8,128,128]{2,1,0:T(8,128)S(1)}, f32[8,128,128]{2,1,0:T(8,128)S(1)}, u32[]{:S(2)}, u32[]{:S(2)}) collective-permute-start(f32[8,128,128]{2,1,0:T(8,128)S(1)} %get-tuple-element.265), channel_id=1, source_target_pairs={{0,1},{1,2},{2,3},{3,4},{4,5},{5,6},{6,7},{7,8},{8,9},{9,10},{10,1... | collective-permute-start | bytes 1572872 | tf_op jit(solution)/shard_map/while/body/eval_jaxpr/ppermute | solution.py:14
  234.6 10.8 %collective-permute-start = (f32[8,128,128]{2,1,0:T(8,128)S(1)}, f32[8,128,128]{2,1,0:T(8,128)S(1)}, u32[]{:S(2)}, u32[]{:S(2)}) collective-permute-start(f32[8,128,128]{2,1,0:T(8,128)S(1)} %get-tuple-element.265), channel_id=1, source_target_pairs={{0,1},{1,2},{2,3},{3,4},{4,5},{5,6},{6,7},{7,8},{8,9},{9,10},{10,1... | collective-permute-start | bytes 1572872 | tf_op jit(solution)/shard_map/while/body/eval_jaxpr/ppermute | solution.py:14
  254.3 10.8 %collective-permute-start = (f32[8,128,128]{2,1,0:T(8,128)S(1)}, f32[8,128,128]{2,1,0:T(8,128)S(1)}, u32[]{:S(2)}, u32[]{:S(2)}) collective-permute-start(f32[8,128,128]{2,1,0:T(8,128)S(1)} %get-tuple-element.265), channel_id=1, source_target_pairs={{0,1},{1,2},{2,3},{3,4},{4,5},{5,6},{6,7},{7,8},{8,9},{9,10},{10,1... | collective-permute-start | bytes 1572872 | tf_op jit(solution)/shard_map/while/body/eval_jaxpr/ppermute | solution.py:14
  273.9 10.8 %collective-permute-start = (f32[8,128,128]{2,1,0:T(8,128)S(1)}, f32[8,128,128]{2,1,0:T(8,128)S(1)}, u32[]{:S(2)}, u32[]{:S(2)}) collective-permute-start(f32[8,128,128]{2,1,0:T(8,128)S(1)} %get-tuple-element.265), channel_id=1, source_target_pairs={{0,1},{1,2},{2,3},{3,4},{4,5},{5,6},{6,7},{7,8},{8,9},{9,10},{10,1... | collective-permute-start | bytes 1572872 | tf_op jit(solution)/shard_map/while/body/eval_jaxpr/ppermute | solution.py:14
  293.5 10.8 %collective-permute-start = (f32[8,128,128]{2,1,0:T(8,128)S(1)}, f32[8,128,128]{2,1,0:T(8,128)S(1)}, u32[]{:S(2)}, u32[]{:S(2)}) collective-permute-start(f32[8,128,128]{2,1,0:T(8,128)S(1)} %get-tuple-element.265), channel_id=1, source_target_pairs={{0,1},{1,2},{2,3},{3,4},{4,5},{5,6},{6,7},{7,8},{8,9},{9,10},{10,1... | collective-permute-start | bytes 1572872 | tf_op jit(solution)/shard_map/while/body/eval_jaxpr/ppermute | solution.py:14
  313.2 10.8 %collective-permute-start = (f32[8,128,128]{2,1,0:T(8,128)S(1)}, f32[8,128,128]{2,1,0:T(8,128)S(1)}, u32[]{:S(2)}, u32[]{:S(2)}) collective-permute-start(f32[8,128,128]{2,1,0:T(8,128)S(1)} %get-tuple-element.265), channel_id=1, source_target_pairs={{0,1},{1,2},{2,3},{3,4},{4,5},{5,6},{6,7},{7,8},{8,9},{9,10},{10,1... | collective-permute-start | bytes 1572872 | tf_op jit(solution)/shard_map/while/body/eval_jaxpr/ppermute | solution.py:14
  332.8 10.8 %collective-permute-start = (f32[8,128,128]{2,1,0:T(8,128)S(1)}, f32[8,128,128]{2,1,0:T(8,128)S(1)}, u32[]{:S(2)}, u32[]{:S(2)}) collective-permute-start(f32[8,128,128]{2,1,0:T(8,128)S(1)} %get-tuple-element.265), channel_id=1, source_target_pairs={{0,1},{1,2},{2,3},{3,4},{4,5},{5,6},{6,7},{7,8},{8,9},{9,10},{10,1... | collective-permute-start | bytes 1572872 | tf_op jit(solution)/shard_map/while/body/eval_jaxpr/ppermute | solution.py:14
  352.5 10.8 %collective-permute-start = (f32[8,128,128]{2,1,0:T(8,128)S(1)}, f32[8,128,128]{2,1,0:T(8,128)S(1)}, u32[]{:S(2)}, u32[]{:S(2)}) collective-permute-start(f32[8,128,128]{2,1,0:T(8,128)S(1)} %get-tuple-element.265), channel_id=1, source_target_pairs={{0,1},{1,2},{2,3},{3,4},{4,5},{5,6},{6,7},{7,8},{8,9},{9,10},{10,1... | collective-permute-start | bytes 1572872 | tf_op jit(solution)/shard_map/while/body/eval_jaxpr/ppermute | solution.py:14
  372.1 10.8 %collective-permute-start = (f32[8,128,128]{2,1,0:T(8,128)S(1)}, f32[8,128,128]{2,1,0:T(8,128)S(1)}, u32[]{:S(2)}, u32[]{:S(2)}) collective-permute-start(f32[8,128,128]{2,1,0:T(8,128)S(1)} %get-tuple-element.265), channel_id=1, source_target_pairs={{0,1},{1,2},{2,3},{3,4},{4,5},{5,6},{6,7},{7,8},{8,9},{9,10},{10,1... | collective-permute-start | bytes 1572872 | tf_op jit(solution)/shard_map/while/body/eval_jaxpr/ppermute | solution.py:14
Sparse Core Ops, SparseCore 0:
  9.7 74.0 all-gather.1
where the time goes:
time: 402 us; the launch traced here: 401 us
  matrix products  237 us (59%)
  waiting for transfers between devices  122 us (30%)
  local copies, waits for them, and re-layouts  16 us (4%)
  between operations  13.5 us (3%)
  other arithmetic  9.96 us (2%)
    dot_general x16, matrix products, add_block(): jnp.einsum('gs,sij->gij', b_pick, b_all, precision=lax.Precision.HIGHEST,...  97 us
    dot_general x16, matrix products, add_block(): jnp.einsum('gij,gjk->gik', left_tiles, right_tiles, precision=lax.Precisi...  73.2 us
    all_gather x1, waiting for transfers between devices, body(): gathered_b = lax.all_gather(b_tiles, 'row', axis=0, tiled=True)  71.7 us
    ppermute x15, waiting for transfers between devices, shifted(): return lax.ppermute(value, axis, pairs)  50.3 us
    dot_general x16, matrix products, add_block(): jnp.einsum('mg,gik->mik', c_place, products, precision=lax.Precision.HIGH...  49.5 us
    dot_general x16, matrix products, add_block(): jnp.einsum('gs,sij->gij', a_pick, a_panel, precision=lax.Precision.HIGHES...  17.2 us
    dynamic_slice x16, local copies, waits for them, and re-layouts, visit(): lax.dynamic_index_in_dim(counts_all, panel_index, 0, keepdims=False)  10.2 us
    lt x16, other arithmetic, add_block(): is_live = jnp.arange(group_size, dtype=jnp.int32) < count_live  9.96 us
  transfers between devices with their start and end apart: 16, of which 16 were waited for; matrix products, arithmetic and copies ran while one was open for 28% of the time, Pallas kernels for 0%

commit v1 on v0

v1 whole, which is shorter than its diff:
```python
import functools

import jax
import jax.numpy as jnp
from jax import lax
from jax.experimental import pallas as pl
from jax.experimental.pallas import tpu as pltpu
from jax.sharding import PartitionSpec as P

CT = 32
BIG = 32
SMALL = 8
CLASSES = 3
LIST = 512 + SMALL
COUNTS = 4 * LIST
A_SLOTS = 128
ZERO_SLOT = A_SLOTS
B_SLOTS = 64
BF = jnp.bfloat16
F32 = jnp.float32


def move_a(value, dy=0, dx=0, dc=0):
    pairs = []
    for i in range(16):
        y, x, c = i // 8, (i // 2) % 4, i % 2
        pairs.append((i, ((y + dy) % 2) * 8 + ((x + dx) % 4) * 2 + (c + dc) % 2))
    return lax.ppermute(value, "col", pairs)


def move_b(value, dy=0, dz=0):
    pairs = []
    for i in range(8):
        y, z = i // 4, i % 4
        pairs.append((i, ((y + dy) % 2) * 4 + (z + dz) % 4))
    return lax.ppermute(value, "row", pairs)


def a_slot(dy, dx, dc):
    return ((dy * 4 + dx) * 2 + dc) * 8


def b_slot(dy, dz):
    return (dy * 4 + dz) * 8


def stage_a(dy, dx):
    return jnp.where((dy == 0) & (dx != 2), 0, jnp.where((dx == 0) | (dy == 0), 1, 2))


def stage_b(dy, dz):
    return jnp.where(dz == 2, 1 + dy, jnp.where((dy == 1) & (dz != 0), 1, 0))


def packed_entries(lists, counts):
    q = lax.axis_index("col")
    r = lax.axis_index("row")
    j = jnp.arange(16, dtype=jnp.int32)[:, None]
    dy, dx, dc = (j // 8) ^ (q // 8), ((j // 2) - (q // 2)) & 3, (j & 1) ^ (q & 1)
    a, b, m = lists[:, 0], lists[:, 1], lists[:, 2]
    part = b >> 3
    by, bz = (part >> 2) ^ (r >> 2), (part - r) & 3
    stage = jnp.maximum(stage_a(dy, dx), stage_b(by, bz))
    live = jnp.arange(32, dtype=jnp.int32)[None, :] < counts[:, None]
    stage = jnp.where(live, stage, CLASSES)
    slot_a = ((dy * 4 + dx) * 2 + dc) * 8 + a
    slot_b = (by * 4 + bz) * 8 + (b & 7)
    return (slot_a | (slot_b << 8) | (m << 14) | (stage << 19)).reshape(-1)


def halves(v):
    hi = v.astype(BF)
    return hi, (v - hi.astype(F32)).astype(BF)


def split_tiles(src, start, count, dst, base):
    def one(i, carry):
        hi, lo = halves(src[start + i])
        dst[base + i, :, :128] = hi
        dst[base + i, :, 128:] = lo
        return carry

    lax.fori_loop(0, count, one, 0, unroll=4)


def prepare_kernel(w_ref, a_ref, b_ref, l_ref, sa, sb, c_ref):
    split_tiles(a_ref, 0, 8, sa, 0)
    split_tiles(b_ref, 0, 8, sb, 0)
    sa[ZERO_SLOT] = jnp.zeros(sa.shape[1:], BF)
    c_ref[...] = jnp.zeros_like(c_ref)

    def step(e, ns):
        w = w_ref[e]
        c = w >> 19
        pos = jnp.where(c == 0, ns[0], jnp.where(c == 1, ns[1], jnp.where(c == 2, ns[2], ns[3])))
        l_ref[pos] = w & 0x7FFFF
        return tuple(ns[k] + (c == k).astype(jnp.int32) for k in range(4))

    start = tuple(jnp.int32(k * LIST) for k in range(4))
    ends = lax.fori_loop(0, 512, step, start, unroll=8)
    for k in range(CLASSES):
        for u in range(SMALL):
            l_ref[ends[k] + u] = jnp.int32(ZERO_SLOT)
        l_ref[COUNTS + k] = ends[k] - k * LIST


STATE = (
    ((A_SLOTS + 1, 128, 256), BF),
    ((B_SLOTS, 128, 256), BF),
    ((CT, 128, 128), F32),
)


def prepare(words, a, b):
    vmem = pl.BlockSpec(memory_space=pltpu.VMEM)
    smem = pl.BlockSpec(memory_space=pltpu.SMEM)
    return pl.pallas_call(
        prepare_kernel,
        out_shape=(jax.ShapeDtypeStruct((COUNTS + CLASSES,), jnp.int32),) + tuple(pltpu.VMEM(*s) for s in STATE),
        in_specs=[smem, vmem, vmem],
        out_specs=(smem, vmem, vmem, vmem),
        name="prepare",
        compiler_params=pltpu.CompilerParams(vmem_limit_bytes=8 * 1024 * 1024),
        cost_estimate=pl.CostEstimate(flops=0, bytes_accessed=16_000_000, transcendentals=0),
    )(words, a, b)


def products_kernel(stage, a_parts, b_parts, n_in, *refs):
    l_ref = refs[0]
    new = refs[1 : 1 + n_in]
    sa_in, sb_in, c_in = refs[1 + n_in : 4 + n_in]
    if stage < CLASSES - 1:
        sa, sb, c_ref = refs[4 + n_in :]
    else:
        sa, sb, c_ref = sa_in, sb_in, refs[4 + n_in]
        sa, sb = refs[5 + n_in :]
        c_ref[...] = c_in[...]
    for k, start, count, base in a_parts:
        split_tiles(new[k], start, count, sa, base)
    for k, start, count, base in b_parts:
        split_tiles(new[k], start, count, sb, base)

    def group(size, first):
        sums, places = [], []
        for u in range(size):
            w = l_ref[first + u]
            right = sb[(w >> 8) & 0x3F]
            r = jnp.dot(sa[w & 0xFF], jnp.concatenate([right, right], axis=0), preferred_element_type=F32)
            sums.append(r[:, :128] + r[:, 128:])
            places.append(w >> 14)
        for s, m in zip(sums, places):
            c_ref[m] = c_ref[m] + s

    base = stage * LIST
    count = l_ref[COUNTS + stage]
    bigs = count // BIG
    rest = (count - bigs * BIG + SMALL - 1) // SMALL

    def big(g, carry):
        group(BIG, base + g * BIG)
        return carry

    def small(g, carry):
        group(SMALL, base + bigs * BIG + g * SMALL)
        return carry

    lax.fori_loop(0, bigs, big, 0)
    lax.fori_loop(0, rest, small, 0)


def products(stage, entries, news, a_parts, b_parts, state, micros):
    n_in = len(news)
    vmem = pl.BlockSpec(memory_space=pltpu.VMEM)
    smem = pl.BlockSpec(memory_space=pltpu.SMEM)
    state = tuple(pltpu.with_memory_space_constraint(s, pltpu.VMEM) for s in state)
    last = stage == CLASSES - 1
    outs = [pltpu.VMEM(*s) for s in STATE]
    aliases = {1 + n_in + i: i for i in range(3)}
    if last:
        outs = [jax.ShapeDtypeStruct(*STATE[2])] + outs[:2]
        aliases = {1 + n_in: 1, 2 + n_in: 2}
    return pl.pallas_call(
        functools.partial(products_kernel, stage, a_parts, b_parts, n_in),
        out_shape=tuple(outs),
        in_specs=[smem] + [vmem] * (n_in + 3),
        out_specs=(vmem,) * 3,
        input_output_aliases=aliases,
        name=f"products_{stage}",
        compiler_params=pltpu.CompilerParams(vmem_limit_bytes=12 * 1024 * 1024),
        cost_estimate=pl.CostEstimate(flops=0, bytes_accessed=micros * 3_000_000, transcendentals=0),
    )(entries, *news, *state)


def after(value, *others):
    return lax.optimization_barrier((value,) + others)[0]


def body(a_tiles, b_tiles, pair_lists, stack_counts):
    a, b = a_tiles[0, 0], b_tiles[0, 0]
    b10, b03, b01 = move_b(b, dy=1), move_b(b, dz=1), move_b(b, dz=-1)
    a03, a01 = move_a(a, dx=1), move_a(a, dx=-1)
    a_late = after(a, b10)
    a10, s00 = move_a(a_late, dy=1), move_a(a_late, dc=1)
    words = packed_entries(pair_lists[0, 0], stack_counts[0, 0])
    entries, *state = prepare(words, a, b)
    a03, a01, b10, b03, b01, entries, *state = lax.optimization_barrier((a03, a01, b10, b03, b01, entries, *state))
    bp = move_b(jnp.concatenate([b10, b03[:4]]), dz=1)
    bm = move_b(jnp.concatenate([b10, b01[4:]]), dz=-1)
    a02p, a02m = move_a(a03[:4], dx=1), move_a(a01[4:], dx=-1)
    a03_late, a01_late, a02p, a02m = lax.optimization_barrier((a03, a01, a02p, a02m))
    s03, s01 = move_a(a03_late, dc=1), move_a(a01_late, dc=1)
    state = products(
        0,
        entries,
        (a03, a01, s00, s03, s01, b03, b01, b10),
        [(0, 0, 8, a_slot(0, 3, 0)), (1, 0, 8, a_slot(0, 1, 0)), (2, 0, 8, a_slot(0, 0, 1)), (3, 0, 8, a_slot(0, 3, 1)), (4, 0, 8, a_slot(0, 1, 1))],
        [(5, 0, 8, b_slot(0, 3)), (6, 0, 8, b_slot(0, 1)), (7, 0, 8, b_slot(1, 0))],
        state,
        8,
    )
    a13, a11 = move_a(a10, dx=1), move_a(a10, dx=-1)
    s10, s02p, s02m = move_a(a10, dc=1), move_a(a02p, dc=1), move_a(a02m, dc=1)
    bp, bm, a10, a02p, a02m, s10, s02p, s02m, *state = lax.optimization_barrier(
        (bp, bm, a10, a02p, a02m, s10, s02p, s02m, *state)
    )
    b12p, b12m = move_b(bp[:4], dz=1), move_b(bm[4:8], dz=-1)
    a12p, a12m = move_a(a13[:4], dx=1), move_a(a11[4:], dx=-1)
    s13, s11 = move_a(a13, dc=1), move_a(a11, dc=1)
    state = products(
        1,
        entries,
        (a10, a02p, a02m, s10, s02p, s02m, bp, bm),
        [
            (3 * c + k, 0, n, slot)
            for c in (0, 1)
            for k, n, slot in ((0, 8, a_slot(1, 0, c)), (1, 4, a_slot(0, 2, c)), (2, 4, a_slot(0, 2, c) + 4))
        ],
        [
            (6, 0, 8, b_slot(1, 3)),
            (6, 8, 4, b_slot(0, 2)),
            (7, 0, 8, b_slot(1, 1)),
            (7, 8, 4, b_slot(0, 2) + 4),
        ],
        state,
        10,
    )
    s12p, s12m = move_a(a12p, dc=1), move_a(a12m, dc=1)
    c = products(
        2,
        entries,
        (a13, a11, a12p, a12m, s13, s11, s12p, s12m, b12p, b12m),
        [
            (4 * c + k, 0, n, slot)
            for c in (0, 1)
            for k, n, slot in (
                (0, 8, a_slot(1, 3, c)),
                (1, 8, a_slot(1, 1, c)),
                (2, 4, a_slot(1, 2, c)),
                (3, 4, a_slot(1, 2, c) + 4),
            )
        ],
        [(8 + h, 0, 4, b_slot(1, 2) + 4 * h) for h in (0, 1)],
        state,
        10,
    )[0]
    return c[None, None]


def solution(mesh):
    return jax.shard_map(
        body,
        mesh=mesh,
        in_specs=(
            P("row", "col", None, None, None),
            P("row", "col", None, None, None),
            P("row", "col", None, None, None),
            P("row", "col", None),
        ),
        out_specs=P("row", "col", None, None, None),
        check_vma=False,
    )
```

time: 402 us -> 88.6 us (0.22)
  the two profiles are of different devices: /device:TPU:0 before, /device:TPU:49 now
where the time goes in v1:
time: 88.6 us; the launch traced here: 88.2 us
  waiting for transfers between devices  35.3 us (40%)
  starting transfers between devices  24.5 us (28%)
  Pallas kernels  23.6 us (27%)
  local copies, waits for them, and re-layouts  2.92 us (3%)
  other arithmetic  1.66 us (2%)
    ppermute x19, waiting for transfers between devices, move_a(): return lax.ppermute(value, 'col', pairs)  25.7 us
    ppermute x19, starting transfers between devices, move_a(): return lax.ppermute(value, 'col', pairs)  19.6 us
    pallas_call x3, Pallas kernels, products(): pl.pallas_call(functools.partial(products_kernel, stage, a_parts, b_parts...  17.9 us
    ppermute x7, waiting for transfers between devices, move_b(): return lax.ppermute(value, 'row', pairs)  9.52 us
    pallas_call x1, Pallas kernels, prepare(): pl.pallas_call(prepare_kernel, out_shape=(jax.ShapeDtypeStruct((COUNTS +...  5.63 us
    ppermute x7, starting transfers between devices, move_b(): return lax.ppermute(value, 'row', pairs)  4.89 us
    unnamed x4, local copies, waits for them, and re-layouts  2.08 us
  transfers between devices with their start and end apart: 26, of which 6 were waited for; matrix products, arithmetic and copies ran while one was open for 3% of the time, Pallas kernels for 17%

profile of v1, /device:TPU:49, one launch (start us, length us, event | category | flops | bytes accessed | tf_op | source)
XLA Modules:
  0.0 88.2 jit_solution(15165720921164468423)
XLA Ops:
  0.0 0.1 collective-permute-start.2
  0.1 1.2 %collective-permute-start = (f32[8,128,128]{2,1,0:T(8,128)}, f32[8,128,128]{2,1,0:T(8,128)S(1)}, u32[]{:S(2)}, u32[]{:S(2)}) collective-permute-start(f32[8,128,128]{2,1,0:T(8,128)} %bitcast.17), channel_id=1, source_target_pairs={{0,2},{1,3},{2,4},{3,5},{4,6},{5,7},{6,0},{7,1},{8,10},{9,11},{10,... | collective-permute-start | bytes 1572872 | tf_op jit(solution)/shard_map/ppermute | solution.py:28
  1.3 1.5 %collective-permute-start.1 = (f32[8,128,128]{2,1,0:T(8,128)}, f32[8,128,128]{2,1,0:T(8,128)S(1)}, u32[]{:S(2)}, u32[]{:S(2)}) collective-permute-start(f32[8,128,128]{2,1,0:T(8,128)} %bitcast.18), channel_id=1, source_target_pairs={{0,6},{1,7},{2,0},{3,1},{4,2},{5,3},{6,4},{7,5},{8,14},{9,15},{10,... | collective-permute-start | bytes 1572872 | tf_op jit(solution)/shard_map/ppermute | solution.py:28
  2.7 1.6 %collective-permute-start.3 = (f32[8,128,128]{2,1,0:T(8,128)}, f32[8,128,128]{2,1,0:T(8,128)S(1)}, u32[]{:S(2)}, u32[]{:S(2)}) collective-permute-start(f32[8,128,128]{2,1,0:T(8,128)} %bitcast.14), channel_id=1, source_target_pairs={{0,16},{16,32},{32,48},{48,0},{64,80},{80,96},{96,112},{112,64},{1... | collective-permute-start | bytes 1572872 | tf_op jit(solution)/shard_map/ppermute | solution.py:36
  4.4 0.0 collective-permute-start.4
  4.4 0.7 fusion.6
  5.1 0.7 iota_compare_fusion
  5.8 8.7 %collective-permute-done.2.refs_8_ = f32[8,128,128]{2,1,0:T(8,128)S(1)} collective-permute-done((f32[8,128,128]{2,1,0:T(8,128)}, f32[8,128,128]{2,1,0:T(8,128)S(1)}, u32[]{:S(2)}, u32[]{:S(2)}) %collective-permute-start.2) | collective-permute-done | bytes 524320 | tf_op jit(solution)/shard_map/ppermute | solution.py:36
  14.5 1.5 %collective-permute-start.21 = (f32[8,128,128]{2,1,0:T(8,128)}, f32[8,128,128]{2,1,0:T(8,128)S(1)}, u32[]{:S(2)}, u32[]{:S(2)}) collective-permute-start(f32[8,128,128]{2,1,0:T(8,128)} %bitcast.19), channel_id=1, source_target_pairs={{0,1},{1,0},{2,3},{3,2},{4,5},{5,4},{6,7},{7,6},{8,9},{9,8},{10,11... | collective-permute-start | bytes 1572872 | tf_op jit(solution)/shard_map/ppermute | solution.py:28
  16.1 0.1 add.64
  16.1 0.1 add.65
  16.2 0.1 max.11
  16.3 0.1 max.12
  16.4 0.1 reshape.146
  16.4 0.1 reshape.147
  16.5 0.1 shift_left.24
  16.6 0.1 squeeze.17
  16.7 0.1 lt.23
  16.8 0.0 copy-start
  16.8 1.0 %copy-done = f32[1,1,8,128,128]{4,3,2,1,0:T(8,128)S(1)} copy-done((f32[1,1,8,128,128]{4,3,2,1,0:T(8,128)S(1)}, f32[1,1,8,128,128]{4,3,2,1,0:T(8,128)}, u32[]{:S(2)}) %copy-start) | copy-done | bytes 524312
  17.8 1.0 %copy-done.1 = f32[1,1,8,128,128]{4,3,2,1,0:T(8,128)S(1)} copy-done((f32[1,1,8,128,128]{4,3,2,1,0:T(8,128)S(1)}, f32[1,1,8,128,128]{4,3,2,1,0:T(8,128)}, u32[]{:S(2)}) %copy-start.1) | copy-done | bytes 524312
  18.9 5.6 %prepare.1 = (s32[2083]{0:T(1024)S(1)}, bf16[129,128,256]{2,1,0:T(8,128)(2,1)S(1)}, bf16[64,128,256]{2,1,0:T(8,128)(2,1)S(1)}, f32[32,128,128]{2,1,0:T(8,128)S(1)}) custom-call(s32[512]{0:T(512)S(1)} %shift-left_or_fusion.w_ref, f32[8,128,128]{2,1,0:T(8,128)S(1)} %bitcast.21, f32[8,128,128]{2,1,0:T(8,128)S(1)} %bitcast.16), custom_call_target="tpu_custom_call" | custom-call | bytes 16000000 | tf_op jit(solution)/shard_map/prepare/pallas_call | solution.py:117
  24.5 0.0 collective-permute-done.refs_1_
  24.5 0.0 collective-permute-done.1.refs_2_
  24.5 0.0 collective-permute-done.3.refs_6_
  24.5 0.0 collective-permute-done.4.refs_7_
  24.6 1.3 %collective-permute-start.16 = (f32[4,128,128]{2,1,0:T(8,128)S(1)}, f32[4,128,128]{2,1,0:T(8,128)S(1)}, u32[]{:S(2)}, u32[]{:S(2)}) collective-permute-start(f32[4,128,128]{2,1,0:T(8,128)S(1)} %slice.40), channel_id=1, source_target_pairs={{0,2},{1,3},{2,4},{3,5},{4,6},{5,7},{6,0},{7,1},{8,10},{9,11},{10,... | collective-permute-start | bytes 786440 | tf_op jit(solution)/shard_map/ppermute | solution.py:28
  25.9 1.5 %collective-permute-start.17 = (f32[4,128,128]{2,1,0:T(8,128)S(1)}, f32[4,128,128]{2,1,0:T(8,128)S(1)}, u32[]{:S(2)}, u32[]{:S(2)}) collective-permute-start(f32[4,128,128]{2,1,0:T(8,128)S(1)} %slice.41), channel_id=1, source_target_pairs={{0,6},{1,7},{2,0},{3,1},{4,2},{5,3},{6,4},{7,5},{8,14},{9,15},{10,... | collective-permute-start | bytes 786440 | tf_op jit(solution)/shard_map/ppermute | solution.py:28
  27.4 6.4 %collective-permute-done.16.refs_2_ = f32[4,128,128]{2,1,0:T(8,128)S(1)} collective-permute-done((f32[4,128,128]{2,1,0:T(8,128)S(1)}, f32[4,128,128]{2,1,0:T(8,128)S(1)}, u32[]{:S(2)}, u32[]{:S(2)}) %collective-permute-start.16) | collective-permute-done | bytes 262176 | tf_op jit(solution)/shard_map/ppermute | solution.py:28
  33.8 0.0 collective-permute-done.17.refs_3_
  33.8 0.9 collective-permute-start.19
  34.7 0.0 collective-permute-start.20
  34.7 1.0 %collective-permute-start.5 = (f32[8,128,128]{2,1,0:T(8,128)}, f32[8,128,128]{2,1,0:T(8,128)S(1)}, u32[]{:S(2)}, u32[]{:S(2)}) collective-permute-start(f32[8,128,128]{2,1,0:T(8,128)} %bitcast.20), channel_id=1, source_target_pairs={{0,8},{1,9},{2,10},{3,11},{4,12},{5,13},{6,14},{7,15},{8,0},{9,1},... | collective-permute-start | bytes 1572872 | tf_op jit(solution)/shard_map/ppermute | solution.py:28
  35.7 0.8 collective-permute-start.22
  36.5 0.0 collective-permute-done.21.refs_3_
  36.5 0.0 collective-permute-start.23
  36.5 0.2 pad_maximum_fusion
  36.7 0.0 collective-permute-done.19.refs_5_
  36.7 1.7 %collective-permute-start.14 = (f32[12,128,128]{2,1,0:T(8,128)S(1)}, f32[12,128,128]{2,1,0:T(8,128)S(1)}, u32[]{:S(2)}, u32[]{:S(2)}) collective-permute-start(f32[12,128,128]{2,1,0:T(8,128)S(1)} %get-tuple-element.78), channel_id=1, source_target_pairs={{0,16},{16,32},{32,48},{48,0},{64,80},{80,96},{96,112},{112,64},{1... | collective-permute-start | bytes 2359304 | tf_op jit(solution)/shard_map/ppermute | solution.py:36
  38.4 0.0 collective-permute-done.20.refs_6_
  38.4 0.0 collective-permute-start.15
  38.4 9.4 %collective-permute-done.5.refs_1_ = f32[8,128,128]{2,1,0:T(8,128)S(1)} collective-permute-done((f32[8,128,128]{2,1,0:T(8,128)}, f32[8,128,128]{2,1,0:T(8,128)S(1)}, u32[]{:S(2)}, u32[]{:S(2)}) %collective-permute-start.5) | collective-permute-done | bytes 524320 | tf_op jit(solution)/shard_map/ppermute | solution.py:28
  47.9 1.4 %collective-permute-start.18 = (f32[8,128,128]{2,1,0:T(8,128)S(1)}, f32[8,128,128]{2,1,0:T(8,128)S(1)}, u32[]{:S(2)}, u32[]{:S(2)}) collective-permute-start(f32[8,128,128]{2,1,0:T(8,128)S(1)} %collective-permute-done.5.refs_1_), channel_id=1, source_target_pairs={{0,1},{1,0},{2,3},{3,2},{4,5},{5,4},{6,7},{7,6},{8,9},{9,8},{10,11... | collective-permute-start | bytes 1572872 | tf_op jit(solution)/shard_map/ppermute | solution.py:28
  49.2 1.2 %collective-permute-start.6 = (f32[8,128,128]{2,1,0:T(8,128)S(1)}, f32[8,128,128]{2,1,0:T(8,128)S(1)}, u32[]{:S(2)}, u32[]{:S(2)}) collective-permute-start(f32[8,128,128]{2,1,0:T(8,128)S(1)} %collective-permute-done.5.refs_1_), channel_id=1, source_target_pairs={{0,2},{1,3},{2,4},{3,5},{4,6},{5,7},{6,0},{7,1},{8,10},{9,11},{10,... | collective-permute-start | bytes 1572872 | tf_op jit(solution)/shard_map/ppermute | solution.py:28
  50.4 1.5 %collective-permute-start.7 = (f32[8,128,128]{2,1,0:T(8,128)S(1)}, f32[8,128,128]{2,1,0:T(8,128)S(1)}, u32[]{:S(2)}, u32[]{:S(2)}) collective-permute-start(f32[8,128,128]{2,1,0:T(8,128)S(1)} %collective-permute-done.5.refs_1_), channel_id=1, source_target_pairs={{0,6},{1,7},{2,0},{3,1},{4,2},{5,3},{6,4},{7,5},{8,14},{9,15},{10,... | collective-permute-start | bytes 1572872 | tf_op jit(solution)/shard_map/ppermute | solution.py:28
  52.0 3.9 %products_0.1 = (bf16[129,128,256]{2,1,0:T(8,128)(2,1)S(1)}, bf16[64,128,256]{2,1,0:T(8,128)(2,1)S(1)}, f32[32,128,128]{2,1,0:T(8,128)S(1)}) custom-call(s32[2083]{0:T(1024)S(1)} %get-tuple-element.45.refs_0_, f32[8,128,128]{2,1,0:T(8,128)S(1)} %collective-permute-done.refs_1_, ...), custom_call_target="tpu_custom_call", output_to_operand_aliasing={{0}: (9, {}), {1}: (10, {}), {2}: (11, {})} | custom-call | bytes 24000000 | tf_op jit(solution)/shard_map/products_0/pallas_call | solution.py:182
  55.8 0.0 collective-permute-done.14.refs_7_
  55.9 0.8 collective-permute-done.15.refs_8_
  56.7 1.4 %collective-permute-start.24 = (f32[4,128,128]{2,1,0:T(8,128)S(1)}, f32[4,128,128]{2,1,0:T(8,128)S(1)}, u32[]{:S(2)}, u32[]{:S(2)}) collective-permute-start(f32[4,128,128]{2,1,0:T(8,128)S(1)} %slice.42), channel_id=1, source_target_pairs={{0,16},{16,32},{32,48},{48,0},{64,80},{80,96},{96,112},{112,64},{1... | collective-permute-start | bytes 786440 | tf_op jit(solution)/shard_map/ppermute | solution.py:36
  58.1 5.9 %collective-permute-done.6.refs_1_ = f32[8,128,128]{2,1,0:T(8,128)S(1)} collective-permute-done((f32[8,128,128]{2,1,0:T(8,128)S(1)}, f32[8,128,128]{2,1,0:T(8,128)S(1)}, u32[]{:S(2)}, u32[]{:S(2)}) %collective-permute-start.6) | collective-permute-done | bytes 524320 | tf_op jit(solution)/shard_map/ppermute | solution.py:28
  64.0 0.1 collective-permute-start.8
  64.1 0.0 collective-permute-done.7.refs_2_
  64.1 2.7 %collective-permute-start.9 = (f32[4,128,128]{2,1,0:T(8,128)S(1)}, f32[4,128,128]{2,1,0:T(8,128)S(1)}, u32[]{:S(2)}, u32[]{:S(2)}) collective-permute-start(f32[4,128,128]{2,1,0:T(8,128)S(1)} %slice.48), channel_id=1, source_target_pairs={{0,6},{1,7},{2,0},{3,1},{4,2},{5,3},{6,4},{7,5},{8,14},{9,15},{10,... | collective-permute-start | bytes 786440 | tf_op jit(solution)/shard_map/ppermute | solution.py:28
  66.9 1.3 %collective-permute-start.10 = (f32[8,128,128]{2,1,0:T(8,128)S(1)}, f32[8,128,128]{2,1,0:T(8,128)S(1)}, u32[]{:S(2)}, u32[]{:S(2)}) collective-permute-start(f32[8,128,128]{2,1,0:T(8,128)S(1)} %collective-permute-done.6.refs_1_), channel_id=1, source_target_pairs={{0,1},{1,0},{2,3},{3,2},{4,5},{5,4},{6,7},{7,6},{8,9},{9,8},{10,11... | collective-permute-start | bytes 1572872 | tf_op jit(solution)/shard_map/ppermute | solution.py:28
  68.2 0.0 collective-permute-start.11
  68.2 0.0 collective-permute-done.24.refs_9_
  68.2 0.1 collective-permute-start.25
  68.3 4.0 %collective-permute-done.8.refs_3_ = f32[4,128,128]{2,1,0:T(8,128)S(1)} collective-permute-done((f32[4,128,128]{2,1,0:T(8,128)S(1)}, f32[4,128,128]{2,1,0:T(8,128)S(1)}, u32[]{:S(2)}, u32[]{:S(2)}) %collective-permute-start.8) | collective-permute-done | bytes 262176 | tf_op jit(solution)/shard_map/ppermute | solution.py:28
  72.4 1.7 %collective-permute-start.12 = (f32[4,128,128]{2,1,0:T(8,128)S(1)}, f32[4,128,128]{2,1,0:T(8,128)S(1)}, u32[]{:S(2)}, u32[]{:S(2)}) collective-permute-start(f32[4,128,128]{2,1,0:T(8,128)S(1)} %collective-permute-done.8.refs_3_), channel_id=1, source_target_pairs={{0,1},{1,0},{2,3},{3,2},{4,5},{5,4},{6,7},{7,6},{8,9},{9,8},{10,11... | collective-permute-start | bytes 786440 | tf_op jit(solution)/shard_map/ppermute | solution.py:28
  74.0 0.0 collective-permute-start.13
  74.0 5.8 %products_1.1 = (bf16[129,128,256]{2,1,0:T(8,128)(2,1)S(1)}, bf16[64,128,256]{2,1,0:T(8,128)(2,1)S(1)}, f32[32,128,128]{2,1,0:T(8,128)S(1)}) custom-call(s32[2083]{0:T(1024)S(1)} %get-tuple-element.45.refs_0_, f32[8,128,128]{2,1,0:T(8,128)S(1)} %collective-permute-done.5.refs_1_, ...), custom_call_target="tpu_custom_call", output_to_operand_aliasing={{0}: (9, {}), {1}: (10, {}), {2}: (11, {})} | custom-call | bytes 30000000 | tf_op jit(solution)/shard_map/products_1/pallas_call | solution.py:182
  79.9 0.0 collective-permute-done.13.refs_8_
  79.9 0.0 collective-permute-done.10.refs_5_
  79.9 8.3 %products_2.1 = (f32[32,128,128]{2,1,0:T(8,128)}, bf16[129,128,256]{2,1,0:T(8,128)(2,1)S(1)}, bf16[64,128,256]{2,1,0:T(8,128)(2,1)S(1)}) custom-call(s32[2083]{0:T(1024)S(1)} %get-tuple-element.45.refs_0_, f32[8,128,128]{2,1,0:T(8,128)S(1)} %collective-permute-done.6.refs_1_, ...), custom_call_target="tpu_custom_call", output_to_operand_aliasing={{1}: (11, {}), {2}: (12, {})} | custom-call | bytes 30000000 | tf_op jit(solution)/shard_map/products_2/pallas_call | solution.py:182
  (18 shorter events, 0.2 us)
Async XLA Ops:
  0.0 14.5 %collective-permute-start.2 = (f32[8,128,128]{2,1,0:T(8,128)}, f32[8,128,128]{2,1,0:T(8,128)S(1)}, u32[]{:S(2)}, u32[]{:S(2)}) collective-permute-start(f32[8,128,128]{2,1,0:T(8,128)} %bitcast.13), channel_id=1, source_target_pairs={{0,64},{16,80},{32,96},{48,112},{64,0},{80,16},{96,32},{112,48},{1... | collective-permute-start | bytes 1572872 | tf_op jit(solution)/shard_map/ppermute | solution.py:36
  0.1 24.5 %collective-permute-start = (f32[8,128,128]{2,1,0:T(8,128)}, f32[8,128,128]{2,1,0:T(8,128)S(1)}, u32[]{:S(2)}, u32[]{:S(2)}) collective-permute-start(f32[8,128,128]{2,1,0:T(8,128)} %bitcast.17), channel_id=1, source_target_pairs={{0,2},{1,3},{2,4},{3,5},{4,6},{5,7},{6,0},{7,1},{8,10},{9,11},{10,... | collective-permute-start | bytes 1572872 | tf_op jit(solution)/shard_map/ppermute | solution.py:28
  1.3 23.3 %collective-permute-start.1 = (f32[8,128,128]{2,1,0:T(8,128)}, f32[8,128,128]{2,1,0:T(8,128)S(1)}, u32[]{:S(2)}, u32[]{:S(2)}) collective-permute-start(f32[8,128,128]{2,1,0:T(8,128)} %bitcast.18), channel_id=1, source_target_pairs={{0,6},{1,7},{2,0},{3,1},{4,2},{5,3},{6,4},{7,5},{8,14},{9,15},{10,... | collective-permute-start | bytes 1572872 | tf_op jit(solution)/shard_map/ppermute | solution.py:28
  2.7 21.8 %collective-permute-start.3 = (f32[8,128,128]{2,1,0:T(8,128)}, f32[8,128,128]{2,1,0:T(8,128)S(1)}, u32[]{:S(2)}, u32[]{:S(2)}) collective-permute-start(f32[8,128,128]{2,1,0:T(8,128)} %bitcast.14), channel_id=1, source_target_pairs={{0,16},{16,32},{32,48},{48,0},{64,80},{80,96},{96,112},{112,64},{1... | collective-permute-start | bytes 1572872 | tf_op jit(solution)/shard_map/ppermute | solution.py:36
  4.4 20.2 %collective-permute-start.4 = (f32[8,128,128]{2,1,0:T(8,128)}, f32[8,128,128]{2,1,0:T(8,128)S(1)}, u32[]{:S(2)}, u32[]{:S(2)}) collective-permute-start(f32[8,128,128]{2,1,0:T(8,128)} %bitcast.15), channel_id=1, source_target_pairs={{0,48},{16,0},{32,16},{48,32},{64,112},{80,64},{96,80},{112,96},{1... | collective-permute-start | bytes 1572872 | tf_op jit(solution)/shard_map/ppermute | solution.py:36
  14.5 22.0 %collective-permute-start.21 = (f32[8,128,128]{2,1,0:T(8,128)}, f32[8,128,128]{2,1,0:T(8,128)S(1)}, u32[]{:S(2)}, u32[]{:S(2)}) collective-permute-start(f32[8,128,128]{2,1,0:T(8,128)} %bitcast.19), channel_id=1, source_target_pairs={{0,1},{1,0},{2,3},{3,2},{4,5},{5,4},{6,7},{7,6},{8,9},{9,8},{10,11... | collective-permute-start | bytes 1572872 | tf_op jit(solution)/shard_map/ppermute | solution.py:28
  16.8 1.0 %copy-start = (f32[1,1,8,128,128]{4,3,2,1,0:T(8,128)S(1)}, f32[1,1,8,128,128]{4,3,2,1,0:T(8,128)}, u32[]{:S(2)}) copy-start(f32[1,1,8,128,128]{4,3,2,1,0:T(8,128)} %param.5) | copy-start | bytes 1572868
  17.8 1.0 %copy-start.1 = (f32[1,1,8,128,128]{4,3,2,1,0:T(8,128)S(1)}, f32[1,1,8,128,128]{4,3,2,1,0:T(8,128)}, u32[]{:S(2)}) copy-start(f32[1,1,8,128,128]{4,3,2,1,0:T(8,128)} %param.4) | copy-start | bytes 1572868
  24.6 9.2 %collective-permute-start.16 = (f32[4,128,128]{2,1,0:T(8,128)S(1)}, f32[4,128,128]{2,1,0:T(8,128)S(1)}, u32[]{:S(2)}, u32[]{:S(2)}) collective-permute-start(f32[4,128,128]{2,1,0:T(8,128)S(1)} %slice.40), channel_id=1, source_target_pairs={{0,2},{1,3},{2,4},{3,5},{4,6},{5,7},{6,0},{7,1},{8,10},{9,11},{10,... | collective-permute-start | bytes 786440 | tf_op jit(solution)/shard_map/ppermute | solution.py:28
  25.9 7.9 %collective-permute-start.17 = (f32[4,128,128]{2,1,0:T(8,128)S(1)}, f32[4,128,128]{2,1,0:T(8,128)S(1)}, u32[]{:S(2)}, u32[]{:S(2)}) collective-permute-start(f32[4,128,128]{2,1,0:T(8,128)S(1)} %slice.41), channel_id=1, source_target_pairs={{0,6},{1,7},{2,0},{3,1},{4,2},{5,3},{6,4},{7,5},{8,14},{9,15},{10,... | collective-permute-start | bytes 786440 | tf_op jit(solution)/shard_map/ppermute | solution.py:28
  33.8 2.9 %collective-permute-start.19 = (f32[4,128,128]{2,1,0:T(8,128)S(1)}, f32[4,128,128]{2,1,0:T(8,128)S(1)}, u32[]{:S(2)}, u32[]{:S(2)}) collective-permute-start(f32[4,128,128]{2,1,0:T(8,128)S(1)} %collective-permute-done.16.refs_2_), channel_id=1, source_target_pairs={{0,1},{1,0},{2,3},{3,2},{4,5},{5,4},{6,7},{7,6},{8,9},{9,8},{10,11... | collective-permute-start | bytes 786440 | tf_op jit(solution)/shard_map/ppermute | solution.py:28
  34.7 3.7 %collective-permute-start.20 = (f32[4,128,128]{2,1,0:T(8,128)S(1)}, f32[4,128,128]{2,1,0:T(8,128)S(1)}, u32[]{:S(2)}, u32[]{:S(2)}) collective-permute-start(f32[4,128,128]{2,1,0:T(8,128)S(1)} %collective-permute-done.17.refs_3_), channel_id=1, source_target_pairs={{0,1},{1,0},{2,3},{3,2},{4,5},{5,4},{6,7},{7,6},{8,9},{9,8},{10,11... | collective-permute-start | bytes 786440 | tf_op jit(solution)/shard_map/ppermute | solution.py:28
  34.7 13.2 %collective-permute-start.5 = (f32[8,128,128]{2,1,0:T(8,128)}, f32[8,128,128]{2,1,0:T(8,128)S(1)}, u32[]{:S(2)}, u32[]{:S(2)}) collective-permute-start(f32[8,128,128]{2,1,0:T(8,128)} %bitcast.20), channel_id=1, source_target_pairs={{0,8},{1,9},{2,10},{3,11},{4,12},{5,13},{6,14},{7,15},{8,0},{9,1},... | collective-permute-start | bytes 1572872 | tf_op jit(solution)/shard_map/ppermute | solution.py:28
  35.7 13.6 %collective-permute-start.22 = (f32[8,128,128]{2,1,0:T(8,128)S(1)}, f32[8,128,128]{2,1,0:T(8,128)S(1)}, u32[]{:S(2)}, u32[]{:S(2)}) collective-permute-start(f32[8,128,128]{2,1,0:T(8,128)S(1)} %collective-permute-done.refs_1_), channel_id=1, source_target_pairs={{0,1},{1,0},{2,3},{3,2},{4,5},{5,4},{6,7},{7,6},{8,9},{9,8},{10,11... | collective-permute-start | bytes 1572872 | tf_op jit(solution)/shard_map/ppermute | solution.py:28
  36.5 14.0 %collective-permute-start.23 = (f32[8,128,128]{2,1,0:T(8,128)S(1)}, f32[8,128,128]{2,1,0:T(8,128)S(1)}, u32[]{:S(2)}, u32[]{:S(2)}) collective-permute-start(f32[8,128,128]{2,1,0:T(8,128)S(1)} %collective-permute-done.1.refs_2_), channel_id=1, source_target_pairs={{0,1},{1,0},{2,3},{3,2},{4,5},{5,4},{6,7},{7,6},{8,9},{9,8},{10,11... | collective-permute-start | bytes 1572872 | tf_op jit(solution)/shard_map/ppermute | solution.py:28
  36.7 19.1 %collective-permute-start.14 = (f32[12,128,128]{2,1,0:T(8,128)S(1)}, f32[12,128,128]{2,1,0:T(8,128)S(1)}, u32[]{:S(2)}, u32[]{:S(2)}) collective-permute-start(f32[12,128,128]{2,1,0:T(8,128)S(1)} %get-tuple-element.78), channel_id=1, source_target_pairs={{0,16},{16,32},{32,48},{48,0},{64,80},{80,96},{96,112},{112,64},{1... | collective-permute-start | bytes 2359304 | tf_op jit(solution)/shard_map/ppermute | solution.py:36
  38.4 18.3 %collective-permute-start.15 = (f32[12,128,128]{2,1,0:T(8,128)S(1)}, f32[12,128,128]{2,1,0:T(8,128)S(1)}, u32[]{:S(2)}, u32[]{:S(2)}) collective-permute-start(f32[12,128,128]{2,1,0:T(8,128)S(1)} %get-tuple-element.77), channel_id=1, source_target_pairs={{0,48},{16,0},{32,16},{48,32},{64,112},{80,64},{96,80},{112,96},{1... | collective-permute-start | bytes 2359304 | tf_op jit(solution)/shard_map/ppermute | solution.py:36
  47.9 8.8 %collective-permute-start.18 = (f32[8,128,128]{2,1,0:T(8,128)S(1)}, f32[8,128,128]{2,1,0:T(8,128)S(1)}, u32[]{:S(2)}, u32[]{:S(2)}) collective-permute-start(f32[8,128,128]{2,1,0:T(8,128)S(1)} %collective-permute-done.5.refs_1_), channel_id=1, source_target_pairs={{0,1},{1,0},{2,3},{3,2},{4,5},{5,4},{6,7},{7,6},{8,9},{9,8},{10,11... | collective-permute-start | bytes 1572872 | tf_op jit(solution)/shard_map/ppermute | solution.py:28
  49.2 14.8 %collective-permute-start.6 = (f32[8,128,128]{2,1,0:T(8,128)S(1)}, f32[8,128,128]{2,1,0:T(8,128)S(1)}, u32[]{:S(2)}, u32[]{:S(2)}) collective-permute-start(f32[8,128,128]{2,1,0:T(8,128)S(1)} %collective-permute-done.5.refs_1_), channel_id=1, source_target_pairs={{0,2},{1,3},{2,4},{3,5},{4,6},{5,7},{6,0},{7,1},{8,10},{9,11},{10,... | collective-permute-start | bytes 1572872 | tf_op jit(solution)/shard_map/ppermute | solution.py:28
  50.4 13.7 %collective-permute-start.7 = (f32[8,128,128]{2,1,0:T(8,128)S(1)}, f32[8,128,128]{2,1,0:T(8,128)S(1)}, u32[]{:S(2)}, u32[]{:S(2)}) collective-permute-start(f32[8,128,128]{2,1,0:T(8,128)S(1)} %collective-permute-done.5.refs_1_), channel_id=1, source_target_pairs={{0,6},{1,7},{2,0},{3,1},{4,2},{5,3},{6,4},{7,5},{8,14},{9,15},{10,... | collective-permute-start | bytes 1572872 | tf_op jit(solution)/shard_map/ppermute | solution.py:28
  56.7 11.5 %collective-permute-start.24 = (f32[4,128,128]{2,1,0:T(8,128)S(1)}, f32[4,128,128]{2,1,0:T(8,128)S(1)}, u32[]{:S(2)}, u32[]{:S(2)}) collective-permute-start(f32[4,128,128]{2,1,0:T(8,128)S(1)} %slice.42), channel_id=1, source_target_pairs={{0,16},{16,32},{32,48},{48,0},{64,80},{80,96},{96,112},{112,64},{1... | collective-permute-start | bytes 786440 | tf_op jit(solution)/shard_map/ppermute | solution.py:36
  64.0 8.3 %collective-permute-start.8 = (f32[4,128,128]{2,1,0:T(8,128)S(1)}, f32[4,128,128]{2,1,0:T(8,128)S(1)}, u32[]{:S(2)}, u32[]{:S(2)}) collective-permute-start(f32[4,128,128]{2,1,0:T(8,128)S(1)} %slice.47), channel_id=1, source_target_pairs={{0,2},{1,3},{2,4},{3,5},{4,6},{5,7},{6,0},{7,1},{8,10},{9,11},{10,... | collective-permute-start | bytes 786440 | tf_op jit(solution)/shard_map/ppermute | solution.py:28
  64.1 9.9 %collective-permute-start.9 = (f32[4,128,128]{2,1,0:T(8,128)S(1)}, f32[4,128,128]{2,1,0:T(8,128)S(1)}, u32[]{:S(2)}, u32[]{:S(2)}) collective-permute-start(f32[4,128,128]{2,1,0:T(8,128)S(1)} %slice.48), channel_id=1, source_target_pairs={{0,6},{1,7},{2,0},{3,1},{4,2},{5,3},{6,4},{7,5},{8,14},{9,15},{10,... | collective-permute-start | bytes 786440 | tf_op jit(solution)/shard_map/ppermute | solution.py:28
  66.9 13.0 %collective-permute-start.10 = (f32[8,128,128]{2,1,0:T(8,128)S(1)}, f32[8,128,128]{2,1,0:T(8,128)S(1)}, u32[]{:S(2)}, u32[]{:S(2)}) collective-permute-start(f32[8,128,128]{2,1,0:T(8,128)S(1)} %collective-permute-done.6.refs_1_), channel_id=1, source_target_pairs={{0,1},{1,0},{2,3},{3,2},{4,5},{5,4},{6,7},{7,6},{8,9},{9,8},{10,11... | collective-permute-start | bytes 1572872 | tf_op jit(solution)/shard_map/ppermute | solution.py:28
  68.2 11.7 %collective-permute-start.11 = (f32[8,128,128]{2,1,0:T(8,128)S(1)}, f32[8,128,128]{2,1,0:T(8,128)S(1)}, u32[]{:S(2)}, u32[]{:S(2)}) collective-permute-start(f32[8,128,128]{2,1,0:T(8,128)S(1)} %collective-permute-done.7.refs_2_), channel_id=1, source_target_pairs={{0,1},{1,0},{2,3},{3,2},{4,5},{5,4},{6,7},{7,6},{8,9},{9,8},{10,11... | collective-permute-start | bytes 1572872 | tf_op jit(solution)/shard_map/ppermute | solution.py:28
  68.2 11.6 %collective-permute-start.25 = (f32[4,128,128]{2,1,0:T(8,128)S(1)}, f32[4,128,128]{2,1,0:T(8,128)S(1)}, u32[]{:S(2)}, u32[]{:S(2)}) collective-permute-start(f32[4,128,128]{2,1,0:T(8,128)S(1)} %slice.43), channel_id=1, source_target_pairs={{0,48},{16,0},{32,16},{48,32},{64,112},{80,64},{96,80},{112,96},{1... | collective-permute-start | bytes 786440 | tf_op jit(solution)/shard_map/ppermute | solution.py:36
  72.4 7.5 %collective-permute-start.12 = (f32[4,128,128]{2,1,0:T(8,128)S(1)}, f32[4,128,128]{2,1,0:T(8,128)S(1)}, u32[]{:S(2)}, u32[]{:S(2)}) collective-permute-start(f32[4,128,128]{2,1,0:T(8,128)S(1)} %collective-permute-done.8.refs_3_), channel_id=1, source_target_pairs={{0,1},{1,0},{2,3},{3,2},{4,5},{5,4},{6,7},{7,6},{8,9},{9,8},{10,11... | collective-permute-start | bytes 786440 | tf_op jit(solution)/shard_map/ppermute | solution.py:28
  74.0 5.8 %collective-permute-start.13 = (f32[4,128,128]{2,1,0:T(8,128)S(1)}, f32[4,128,128]{2,1,0:T(8,128)S(1)}, u32[]{:S(2)}, u32[]{:S(2)}) collective-permute-start(f32[4,128,128]{2,1,0:T(8,128)S(1)} %collective-permute-done.9.refs_4_), channel_id=1, source_target_pairs={{0,1},{1,0},{2,3},{3,2},{4,5},{5,4},{6,7},{7,6},{8,9},{9,8},{10,11... | collective-permute-start | bytes 786440 | tf_op jit(solution)/shard_map/ppermute | solution.py:28

commit v2 on v1

v2 whole, which is shorter than its diff:
```python
import functools

import jax
import jax.numpy as jnp
from jax import lax
from jax.experimental import pallas as pl
from jax.experimental.pallas import tpu as pltpu
from jax.sharding import PartitionSpec as P

CT = 32
BIG = 32
SMALL = 8
CLASSES = 5
LIST = 512 + SMALL
COUNTS = (CLASSES + 1) * LIST
A_SLOTS = 128
ZERO_SLOT = A_SLOTS
B_SLOTS = 64
BF = jnp.bfloat16
F32 = jnp.float32


def move_a(value, dy=0, dx=0, dc=0):
    pairs = []
    for i in range(16):
        y, x, c = i // 8, (i // 2) % 4, i % 2
        pairs.append((i, ((y + dy) % 2) * 8 + ((x + dx) % 4) * 2 + (c + dc) % 2))
    return lax.ppermute(value, "col", pairs)


def move_b(value, dy=0, dz=0):
    pairs = []
    for i in range(8):
        y, z = i // 4, i % 4
        pairs.append((i, ((y + dy) % 2) * 4 + (z + dz) % 4))
    return lax.ppermute(value, "row", pairs)


def a_slot(dy, dx, dc):
    return ((dy * 4 + dx) * 2 + dc) * 8


def b_slot(dy, dz):
    return (dy * 4 + dz) * 8


def stage_of(dy, dx, dc, by, bz):
    far_b = (by == 1) & (bz != 0)
    stage = jnp.where(far_b, 2, dc)
    stage = jnp.where(dx == 2, 3, stage)
    return jnp.where(far_b & (bz == 2), 4, stage)


def packed_entries(lists, counts):
    q = lax.axis_index("col")
    r = lax.axis_index("row")
    j = jnp.arange(16, dtype=jnp.int32)[:, None]
    dy, dx, dc = (j // 8) ^ (q // 8), ((j // 2) - (q // 2)) & 3, (j & 1) ^ (q & 1)
    a, b, m = lists[:, 0], lists[:, 1], lists[:, 2]
    part = b >> 3
    by, bz = (part >> 2) ^ (r >> 2), (part - r) & 3
    stage = stage_of(dy, dx, dc, by, bz)
    live = jnp.arange(32, dtype=jnp.int32)[None, :] < counts[:, None]
    stage = jnp.where(live, stage, CLASSES)
    slot_a = ((dy * 4 + dx) * 2 + dc) * 8 + a
    slot_b = (by * 4 + bz) * 8 + (b & 7)
    return (slot_a | (slot_b << 8) | (m << 14) | (stage << 19)).reshape(-1)


def halves(v):
    hi = v.astype(BF)
    return hi, (v - hi.astype(F32)).astype(BF)


def split_tiles(src, start, count, dst, base):
    def one(i, carry):
        hi, lo = halves(src[start + i])
        dst[base + i, :, :128] = hi
        dst[base + i, :, 128:] = lo
        return carry

    lax.fori_loop(0, count, one, 0, unroll=4)


def sort_kernel(w_ref, words_ref, l_ref, rank_ref, place_ref, counts, places, sems):
    kinds = jnp.broadcast_to(words_ref[...] >> 19, (8, 512))
    is_kind = kinds == lax.broadcasted_iota(jnp.int32, (8, 512), 0)
    before = lax.broadcasted_iota(jnp.int32, (512, 512), 0) <= lax.broadcasted_iota(jnp.int32, (512, 512), 1)
    ones = jnp.where(is_kind, 1.0, 0.0).astype(BF)
    triangle = jnp.where(before, 1.0, 0.0).astype(BF)
    rank = jnp.dot(ones, triangle, preferred_element_type=F32).astype(jnp.int32)
    rank_ref[...] = rank
    starts = lax.broadcasted_iota(jnp.int32, (8, 512), 0) * LIST
    place_ref[...] = jnp.sum(jnp.where(is_kind, starts + rank - 1, 0), axis=0, keepdims=True)
    copies = [
        pltpu.make_async_copy(rank_ref, counts, sems.at[0]),
        pltpu.make_async_copy(place_ref, places, sems.at[1]),
    ]
    for copy in copies:
        copy.start()
    for copy in copies:
        copy.wait()

    def store(e, carry):
        l_ref[places[0, e]] = w_ref[e] & 0x7FFFF
        return carry

    lax.fori_loop(0, 512, store, 0, unroll=16)
    for k in range(CLASSES):
        count = counts[k, 511]
        for u in range(SMALL):
            l_ref[k * LIST + count + u] = jnp.int32(ZERO_SLOT)
        l_ref[COUNTS + k] = count


def sort_entries(words):
    smem = pl.BlockSpec(memory_space=pltpu.SMEM)
    return pl.pallas_call(
        sort_kernel,
        out_shape=jax.ShapeDtypeStruct((COUNTS + CLASSES,), jnp.int32),
        in_specs=[smem, pl.BlockSpec(memory_space=pltpu.VMEM)],
        out_specs=smem,
        scratch_shapes=[
            pltpu.VMEM((8, 512), jnp.int32),
            pltpu.VMEM((1, 512), jnp.int32),
            pltpu.SMEM((8, 512), jnp.int32),
            pltpu.SMEM((1, 512), jnp.int32),
            pltpu.SemaphoreType.DMA((2,)),
        ],
        name="sort_entries",
        cost_estimate=pl.CostEstimate(flops=0, bytes_accessed=16_000_000, transcendentals=0),
    )(words, words.reshape(1, 512))


STATE = (
    ((A_SLOTS + 1, 128, 256), BF),
    ((B_SLOTS, 128, 256), BF),
    ((CT, 128, 128), F32),
)


def split_kernel(n_in, a_parts, b_parts, *refs):
    news, (sa, sb, c_ref) = refs[:n_in], refs[n_in : n_in + 3]
    a_hbm, b_hbm = news[:2]
    a_ref, b_ref, sems = refs[n_in + 3 :]
    copies = [
        pltpu.make_async_copy(a_hbm, a_ref, sems.at[0]),
        pltpu.make_async_copy(b_hbm, b_ref, sems.at[1]),
    ]
    for copy in copies:
        copy.start()
    sa[ZERO_SLOT] = jnp.zeros(sa.shape[1:], BF)
    c_ref[...] = jnp.zeros_like(c_ref)
    for k, start, count, base in a_parts:
        split_tiles(news[k], start, count, sa, base)
    for k, start, count, base in b_parts:
        split_tiles(news[k], start, count, sb, base)
    for copy in copies:
        copy.wait()
    split_tiles(a_ref, 0, 8, sa, a_slot(0, 0, 0))
    split_tiles(b_ref, 0, 8, sb, b_slot(0, 0))


def first_splits(news, a_parts, b_parts):
    vmem = pl.BlockSpec(memory_space=pltpu.VMEM)
    hbm = pl.BlockSpec(memory_space=pl.ANY)
    own = tuple(pltpu.with_memory_space_constraint(v, pltpu.HBM) for v in news[:2])
    return pl.pallas_call(
        functools.partial(split_kernel, len(news), a_parts, b_parts),
        out_shape=tuple(pltpu.VMEM(*s) for s in STATE),
        in_specs=[hbm] * 2 + [vmem] * (len(news) - 2),
        out_specs=(vmem,) * 3,
        scratch_shapes=[pltpu.VMEM((8, 128, 128), F32)] * 2 + [pltpu.SemaphoreType.DMA((2,))],
        name="first_splits",
        compiler_params=pltpu.CompilerParams(vmem_limit_bytes=8 * 1024 * 1024),
        cost_estimate=pl.CostEstimate(flops=0, bytes_accessed=4_000_000, transcendentals=0),
    )(*own, *news[2:])


def more_splits_kernel(n_in, a_parts, b_parts, *refs):
    news, (sa, sb) = refs[:n_in], refs[n_in + 2 :]
    for k, start, count, base in a_parts:
        split_tiles(news[k], start, count, sa, base)
    for k, start, count, base in b_parts:
        split_tiles(news[k], start, count, sb, base)


def more_splits(news, a_parts, b_parts, state):
    vmem = pl.BlockSpec(memory_space=pltpu.VMEM)
    tiles = tuple(pltpu.with_memory_space_constraint(s, pltpu.VMEM) for s in state[:2])
    news = tuple(pltpu.with_memory_space_constraint(s, pltpu.VMEM) for s in news)
    sa, sb = pl.pallas_call(
        functools.partial(more_splits_kernel, len(news), a_parts, b_parts),
        out_shape=tuple(pltpu.VMEM(*s) for s in STATE[:2]),
        in_specs=[vmem] * (len(news) + 2),
        out_specs=(vmem,) * 2,
        input_output_aliases={len(news) + i: i for i in range(2)},
        name="more_splits",
        compiler_params=pltpu.CompilerParams(vmem_limit_bytes=8 * 1024 * 1024),
        cost_estimate=pl.CostEstimate(flops=0, bytes_accessed=4_000_000, transcendentals=0),
    )(*news, *tiles)
    return sa, sb, state[2]


def products_kernel(stage, a_parts, b_parts, n_in, *refs):
    l_ref = refs[0]
    new = refs[1 : 1 + n_in]
    sa_in, sb_in, c_in = refs[1 + n_in : 4 + n_in]
    sa, sb, c_ref = refs[4 + n_in : 7 + n_in]
    for k, start, count, base in a_parts:
        split_tiles(new[k], start, count, sa, base)
    for k, start, count, base in b_parts:
        split_tiles(new[k], start, count, sb, base)

    def group(size, first):
        sums, places = [], []
        for u in range(size):
            w = l_ref[first + u]
            right = sb[(w >> 8) & 0x3F]
            r = jnp.dot(sa[w & 0xFF], jnp.concatenate([right, right], axis=0), preferred_element_type=F32)
            sums.append(r[:, :128] + r[:, 128:])
            places.append(w >> 14)
        for s, m in zip(sums, places):
            c_ref[m] = c_ref[m] + s

    base = stage * LIST
    count = l_ref[COUNTS + stage]
    bigs = count // BIG
    rest = (count - bigs * BIG + SMALL - 1) // SMALL

    def big(g, carry):
        group(BIG, base + g * BIG)
        return carry

    def small(g, carry):
        group(SMALL, base + bigs * BIG + g * SMALL)
        return carry

    lax.fori_loop(0, bigs, big, 0)
    lax.fori_loop(0, rest, small, 0)
    if stage == CLASSES - 1:
        out_hbm, sem = refs[7 + n_in :]
        copy = pltpu.make_async_copy(c_ref, out_hbm, sem)
        copy.start()
        copy.wait()


def products(stage, entries, news, a_parts, b_parts, state, micros):
    n_in = len(news)
    vmem = pl.BlockSpec(memory_space=pltpu.VMEM)
    smem = pl.BlockSpec(memory_space=pltpu.SMEM)
    state = tuple(pltpu.with_memory_space_constraint(s, pltpu.VMEM) for s in state)
    news = tuple(pltpu.with_memory_space_constraint(s, pltpu.VMEM) for s in news)
    last = stage == CLASSES - 1
    outs = [pltpu.VMEM(*s) for s in STATE]
    aliases = {1 + n_in + i: i for i in range(3)}
    out_specs, scratch = (vmem,) * 3, []
    if last:
        outs += [pltpu.HBM(*STATE[2])]
        out_specs += (pl.BlockSpec(memory_space=pltpu.HBM),)
        scratch = [pltpu.SemaphoreType.DMA(())]
    return pl.pallas_call(
        functools.partial(products_kernel, stage, a_parts, b_parts, n_in),
        out_shape=tuple(outs),
        in_specs=[smem] + [vmem] * (n_in + 3),
        out_specs=out_specs,
        scratch_shapes=scratch,
        input_output_aliases=aliases,
        name=f"products_{stage}",
        compiler_params=pltpu.CompilerParams(vmem_limit_bytes=12 * 1024 * 1024),
        cost_estimate=pl.CostEstimate(flops=5 * 10**10, bytes_accessed=1, transcendentals=0),
    )(entries, *news, *state)


def body(a_tiles, b_tiles, pair_lists, stack_counts):
    barrier = lax.optimization_barrier
    a, b = a_tiles[0, 0], b_tiles[0, 0]
    a10, a03, a01 = move_a(a, dy=1), move_a(a, dx=1), move_a(a, dx=-1)
    words = packed_entries(pair_lists[0, 0], stack_counts[0, 0])
    words, b_late = barrier((words, b))
    b03, b01 = move_b(b_late, dz=1), move_b(b_late, dz=-1)
    entries = sort_entries(words)
    a10, a03, a01, entries, a, b = barrier((a10, a03, a01, entries, a, b))
    b10 = move_b(b, dy=1)
    a13, a11 = move_a(a10, dx=1), move_a(a10, dx=-1)
    state = first_splits(
        (a, b, a10, a03, a01),
        [(2, 0, 8, a_slot(1, 0, 0)), (3, 0, 8, a_slot(0, 3, 0)), (4, 0, 8, a_slot(0, 1, 0))],
        [],
    )
    b03, b01, *state = barrier((b03, b01, *state))
    b02p, b02m = move_b(b03[:4], dz=1), move_b(b01[4:], dz=-1)
    b10, b02p, b02m = barrier((b10, b02p, b02m))
    b13, b11 = move_b(b10, dz=1), move_b(b10, dz=-1)
    state = more_splits(
        (a13, a11, b03, b01, b10, b02p, b02m),
        [(0, 0, 8, a_slot(1, 3, 0)), (1, 0, 8, a_slot(1, 1, 0))],
        [
            (2, 0, 8, b_slot(0, 3)),
            (3, 0, 8, b_slot(0, 1)),
            (4, 0, 8, b_slot(1, 0)),
            (5, 0, 4, b_slot(0, 2)),
            (6, 0, 4, b_slot(0, 2) + 4),
        ],
        state,
    )
    a, a10, a03, a01, a13, a11, *state = barrier((a, a10, a03, a01, a13, a11, *state))
    ap = move_a(jnp.concatenate([a03[:4], a13[:4]]), dx=1)
    am = move_a(jnp.concatenate([a01[4:], a11[4:]]), dx=-1)
    near = move_a(jnp.concatenate([a, a10, a03, a01, a13, a11]), dc=1)
    state = products(0, entries, (), [], [], state, 3)
    state = products(
        1,
        entries,
        (near,),
        [
            (0, 8 * k, 8, a_slot(dy, dx, 1))
            for k, (dy, dx) in enumerate(((0, 0), (1, 0), (0, 3), (0, 1), (1, 3), (1, 1)))
        ],
        [],
        state,
        4,
    )
    b13, b11, *state = barrier((b13, b11, *state))
    b12p, b12m = move_b(b13[:4], dz=1), move_b(b11[4:], dz=-1)
    ap, am, b13, b11 = barrier((ap, am, b13, b11))
    far = move_a(jnp.concatenate([ap, am]), dc=1)
    state = products(
        2,
        entries,
        (ap, am, b13, b11),
        [(h, 4 * dy, 4, a_slot(dy, 2, 0) + 4 * h) for h in (0, 1) for dy in (0, 1)],
        [(2, 0, 8, b_slot(1, 3)), (3, 0, 8, b_slot(1, 1))],
        state,
        3,
    )
    state = products(
        3,
        entries,
        (far,),
        [(0, 8 * h + 4 * dy, 4, a_slot(dy, 2, 1) + 4 * h) for h in (0, 1) for dy in (0, 1)],
        [],
        state,
        3,
    )
    c = products(
        4,
        entries,
        (b12p, b12m),
        [],
        [(h, 0, 4, b_slot(1, 2) + 4 * h) for h in (0, 1)],
        state,
        2,
    )[3]
    return c[None, None]


def solution(mesh):
    return jax.shard_map(
        body,
        mesh=mesh,
        in_specs=(
            P("row", "col", None, None, None),
            P("row", "col", None, None, None),
            P("row", "col", None, None, None),
            P("row", "col", None),
        ),
        out_specs=P("row", "col", None, None, None),
        check_vma=False,
    )
```

time: 88.6 us -> 66.7 us (0.75)
  the two profiles are of different devices: /device:TPU:49 before, /device:TPU:0 now
where the time goes in v2:
time: 66.7 us; the launch traced here: 66.4 us
  Pallas kernels  24.8 us (37%)
  starting transfers between devices  23.2 us (35%)
  waiting for transfers between devices  13.6 us (20%)
  other arithmetic  2.93 us (4%)
  local copies, waits for them, and re-layouts  1.59 us (2%)
    pallas_call x5, Pallas kernels, products(): pl.pallas_call(functools.partial(products_kernel, stage, a_parts, b_parts...  19.5 us
    ppermute x9, starting transfers between devices, move_b(): return lax.ppermute(value, 'row', pairs)  13.5 us
    ppermute x9, starting transfers between devices, move_a(): return lax.ppermute(value, 'col', pairs)  9.71 us
    ppermute x9, waiting for transfers between devices, move_b(): return lax.ppermute(value, 'row', pairs)  9.71 us
    ppermute x9, waiting for transfers between devices, move_a(): return lax.ppermute(value, 'col', pairs)  3.9 us
    pallas_call x1, Pallas kernels, sort_entries(): pl.pallas_call(sort_kernel, out_shape=jax.ShapeDtypeStruct((COUNTS + CLAS...  3.37 us
    pallas_call x1, Pallas kernels, first_splits(): pl.pallas_call(functools.partial(split_kernel, len(news), a_parts, b_part...  1.39 us
  transfers between devices with their start and end apart: 18, of which 6 were waited for; matrix products, arithmetic and copies ran while one was open for 6% of the time, Pallas kernels for 31%

profile of v2, /device:TPU:0, one launch (start us, length us, event | category | flops | bytes accessed | tf_op | source)
XLA Modules:
  0.0 66.4 jit_solution(3396645934795506208)
XLA Ops:
  0.0 2.8 %collective-permute-start.2 = (f32[8,128,128]{2,1,0:T(8,128)}, f32[8,128,128]{2,1,0:T(8,128)S(1)}, u32[]{:S(2)}, u32[]{:S(2)}) collective-permute-start(f32[8,128,128]{2,1,0:T(8,128)} %bitcast.16), channel_id=1, source_target_pairs={{0,6},{1,7},{2,0},{3,1},{4,2},{5,3},{6,4},{7,5},{8,14},{9,15},{10,... | collective-permute-start | bytes 1572872 | tf_op jit(solution)/shard_map/ppermute | solution.py:28
  2.8 0.0 collective-permute-start.1
  2.8 1.6 %collective-permute-start = (f32[8,128,128]{2,1,0:T(8,128)}, f32[8,128,128]{2,1,0:T(8,128)S(1)}, u32[]{:S(2)}, u32[]{:S(2)}) collective-permute-start(f32[8,128,128]{2,1,0:T(8,128)} %bitcast.18), channel_id=1, source_target_pairs={{0,8},{1,9},{2,10},{3,11},{4,12},{5,13},{6,14},{7,15},{8,0},{9,1},... | collective-permute-start | bytes 1572872 | tf_op jit(solution)/shard_map/ppermute | solution.py:28
  4.4 0.7 %fusion = (pred[16,1,32]{2,0,1:T(8,128)(4,1)S(1)}, pred[16,1,32]{2,0,1:T(8,128)(4,1)S(1)}) fusion(s32[16,3,32]{2,0,1:T(8,128)} %bitcast.25, s32[]{:T(128)S(6)} %axis_index.25, s32[]{:T(128)S(6)} %shift_right_arithmetic.15), kind=kLoop, calls=%fused_computation.16 | loop fusion | flops 4608 | bytes 3080 | tf_op jit(solution)/shard_map/eq | solution.py:51
  5.1 0.7 %fusion.10 = (s32[16,1,32]{2,0,1:T(8,128)S(1)}, s32[16,1,32]{2,0,1:T(8,128)S(1)}, s32[16,1,32]{2,0,1:T(8,128)S(1)}) fusion(s32[16,3,32]{2,0,1:T(8,128)} %bitcast.26, s32[]{:T(128)S(6)} %axis_index.25, s32[]{:T(128)S(6)} %shift_right_arithmetic.15), kind=kLoop, calls=%fused_computation.35 | loop fusion | flops 6144 | bytes 12296 | tf_op jit(solution)/shard_map/slice | solution.py:59
  5.9 0.7 %iota_compare_fusion = pred[16,32]{1,0:T(8,128)(4,1)S(1)} fusion(s32[16]{0:T(128)} %bitcast.28), kind=kLoop, calls=%fused_computation.11 | loop fusion | flops 512 | bytes 576 | tf_op jit(solution)/shard_map/lt | solution.py:63
  6.6 0.1 broadcast_in_dim.35
  6.7 0.1 broadcast_in_dim.36
  6.8 0.1 lt.23
  6.9 0.1 reshape.129
  7.0 0.1 reshape.132
  7.1 0.1 broadcast_in_dim.37
  7.1 0.1 broadcast_in_dim.38
  7.2 0.1 add.54
  7.3 0.1 add.55
  7.4 0.1 squeeze.16
  7.4 0.1 reshape.135
  7.5 0.1 shift_left.24
  7.6 0.6 shift-left_or_fusion.w_ref
  8.2 4.0 %collective-permute-start.5 = (f32[8,128,128]{2,1,0:T(8,128)}, f32[8,128,128]{2,1,0:T(8,128)S(1)}, u32[]{:S(2)}, u32[]{:S(2)}) collective-permute-start(f32[8,128,128]{2,1,0:T(8,128)} %bitcast.21), channel_id=1, source_target_pairs={{0,48},{16,0},{32,16},{48,32},{64,112},{80,64},{96,80},{112,96},{1... | collective-permute-start | bytes 1572872 | tf_op jit(solution)/shard_map/ppermute | solution.py:36
  12.2 0.0 collective-permute-start.4
  12.2 3.4 %sort_entries.1.refs_0_ = s32[3125]{0:T(1024)} custom-call(s32[512]{0:T(512)} %shift-left_or_fusion.w_ref, s32[1,512]{1,0:T(1,128)} %bitcast.27), custom_call_target="tpu_custom_call" | custom-call | bytes 16000000 | tf_op jit(solution)/shard_map/sort_entries/pallas_call | solution.py:118
  15.6 0.0 collective-permute-done.2.refs_4_
  15.6 2.0 %collective-permute-done.1.refs_3_ = f32[8,128,128]{2,1,0:T(8,128)S(1)} collective-permute-done((f32[8,128,128]{2,1,0:T(8,128)}, f32[8,128,128]{2,1,0:T(8,128)S(1)}, u32[]{:S(2)}, u32[]{:S(2)}) %collective-permute-start.1) | collective-permute-done | bytes 524320 | tf_op jit(solution)/shard_map/ppermute | solution.py:28
  17.6 0.0 collective-permute-done.refs_2_
  17.7 3.2 %collective-permute-start.3 = (f32[8,128,128]{2,1,0:T(8,128)}, f32[8,128,128]{2,1,0:T(8,128)S(1)}, u32[]{:S(2)}, u32[]{:S(2)}) collective-permute-start(f32[8,128,128]{2,1,0:T(8,128)} %bitcast.23), channel_id=1, source_target_pairs={{0,64},{16,80},{32,96},{48,112},{64,0},{80,16},{96,32},{112,48},{1... | collective-permute-start | bytes 1572872 | tf_op jit(solution)/shard_map/ppermute | solution.py:36
  20.8 1.7 %collective-permute-start.11 = (f32[8,128,128]{2,1,0:T(8,128)S(1)}, f32[8,128,128]{2,1,0:T(8,128)S(1)}, u32[]{:S(2)}, u32[]{:S(2)}) collective-permute-start(f32[8,128,128]{2,1,0:T(8,128)S(1)} %collective-permute-done.refs_2_), channel_id=1, source_target_pairs={{0,6},{1,7},{2,0},{3,1},{4,2},{5,3},{6,4},{7,5},{8,14},{9,15},{10,... | collective-permute-start | bytes 1572872 | tf_op jit(solution)/shard_map/ppermute | solution.py:28
  22.6 0.3 collective-permute-start.10
  22.9 1.4 %first_splits.1 = (bf16[129,128,256]{2,1,0:T(8,128)(2,1)S(1)}, bf16[64,128,256]{2,1,0:T(8,128)(2,1)S(1)}, f32[32,128,128]{2,1,0:T(8,128)S(1)}) custom-call(f32[8,128,128]{2,1,0:T(8,128)} %bitcast.19, f32[8,128,128]{2,1,0:T(8,128)} %bitcast.24, f32[8,128,128]{2,1,0:T(8,128)S(1)} %collective-permute-done.refs_2_, ...), custom_call_target="tpu_custom_call" | custom-call | bytes 4000000 | tf_op jit(solution)/shard_map/first_splits/pallas_call | solution.py:168
  24.3 0.0 collective-permute-done.5.refs_3_
  24.3 2.2 %collective-permute-done.4.refs_2_ = f32[8,128,128]{2,1,0:T(8,128)S(1)} collective-permute-done((f32[8,128,128]{2,1,0:T(8,128)}, f32[8,128,128]{2,1,0:T(8,128)S(1)}, u32[]{:S(2)}, u32[]{:S(2)}) %collective-permute-start.4) | collective-permute-done | bytes 524320 | tf_op jit(solution)/shard_map/ppermute | solution.py:36
  26.5 1.9 %collective-permute-start.7 = (f32[4,128,128]{2,1,0:T(8,128)S(1)}, f32[4,128,128]{2,1,0:T(8,128)S(1)}, u32[]{:S(2)}, u32[]{:S(2)}) collective-permute-start(f32[4,128,128]{2,1,0:T(8,128)S(1)} %slice.37), channel_id=1, source_target_pairs={{0,48},{16,0},{32,16},{48,32},{64,112},{80,64},{96,80},{112,96},{1... | collective-permute-start | bytes 786440 | tf_op jit(solution)/shard_map/ppermute | solution.py:36
  28.5 0.2 collective-permute-start.6
  28.6 4.3 %collective-permute-done.7.refs_6_ = f32[4,128,128]{2,1,0:T(8,128)S(1)} collective-permute-done((f32[4,128,128]{2,1,0:T(8,128)S(1)}, f32[4,128,128]{2,1,0:T(8,128)S(1)}, u32[]{:S(2)}, u32[]{:S(2)}) %collective-permute-start.7) | collective-permute-done | bytes 262176 | tf_op jit(solution)/shard_map/ppermute | solution.py:36
  33.0 3.1 %collective-permute-done.6.refs_5_ = f32[4,128,128]{2,1,0:T(8,128)S(1)} collective-permute-done((f32[4,128,128]{2,1,0:T(8,128)S(1)}, f32[4,128,128]{2,1,0:T(8,128)S(1)}, u32[]{:S(2)}, u32[]{:S(2)}) %collective-permute-start.6) | collective-permute-done | bytes 262176 | tf_op jit(solution)/shard_map/ppermute | solution.py:36
  36.0 0.0 collective-permute-done.3.refs_4_
  36.0 0.0 collective-permute-start.9
  36.0 2.0 %collective-permute-start.8 = (f32[8,128,128]{2,1,0:T(8,128)S(1)}, f32[8,128,128]{2,1,0:T(8,128)S(1)}, u32[]{:S(2)}, u32[]{:S(2)}) collective-permute-start(f32[8,128,128]{2,1,0:T(8,128)S(1)} %collective-permute-done.3.refs_4_), channel_id=1, source_target_pairs={{0,16},{16,32},{32,48},{48,0},{64,80},{80,96},{96,112},{112,64},{1... | collective-permute-start | bytes 1572872 | tf_op jit(solution)/shard_map/ppermute | solution.py:36
  38.1 0.0 collective-permute-done.11.refs_1_
  38.1 0.0 collective-permute-done.10.refs_0_
  38.1 0.5 more_splits.1
  38.6 0.0 copy-start.1
  38.8 3.0 %collective-permute-start.16 = (f32[8,128,128]{2,1,0:T(8,128)S(1)}, f32[8,128,128]{2,1,0:T(8,128)S(1)}, u32[]{:S(2)}, u32[]{:S(2)}) collective-permute-start(f32[8,128,128]{2,1,0:T(8,128)S(1)} %pad_maximum_fusion.2), channel_id=1, source_target_pairs={{0,6},{1,7},{2,0},{3,1},{4,2},{5,3},{6,4},{7,5},{8,14},{9,15},{10,... | collective-permute-start | bytes 1572872 | tf_op jit(solution)/shard_map/ppermute | solution.py:28
  41.8 0.0 copy-start
  41.9 0.1 collective-permute-start.15
  42.2 0.1 collective-permute-start.12
  42.3 0.3 copy-done
  42.6 3.5 %products_0.1 = (bf16[129,128,256]{2,1,0:T(8,128)(2,1)S(1)}, bf16[64,128,256]{2,1,0:T(8,128)(2,1)S(1)}, f32[32,128,128]{2,1,0:T(8,128)S(1)}) custom-call(s32[3125]{0:T(1024)S(1)} %copy-done, bf16[129,128,256]{2,1,0:T(8,128)(2,1)S(1)} %get-tuple-element.84.refs_1_, ...), custom_call_target="tpu_custom_call", output_to_operand_aliasing={{0}: (1, {}), {1}: (2, {}), {2}: (3, {})} | custom-call | flops 49999998976 | bytes 1 | tf_op jit(solution)/shard_map/products_0/pallas_call | solution.py:262
  46.1 1.9 %collective-permute-done.12.refs_1_ = f32[48,128,128]{2,1,0:T(8,128)S(1)} collective-permute-done((f32[48,128,128]{2,1,0:T(8,128)S(1)}, f32[48,128,128]{2,1,0:T(8,128)S(1)}, u32[]{:S(2)}, u32[]{:S(2)}) %collective-permute-start.12) | collective-permute-done | bytes 3145760 | tf_op jit(solution)/shard_map/ppermute | solution.py:28
  48.0 4.5 %products_1.1 = (bf16[129,128,256]{2,1,0:T(8,128)(2,1)S(1)}, bf16[64,128,256]{2,1,0:T(8,128)(2,1)S(1)}, f32[32,128,128]{2,1,0:T(8,128)S(1)}) custom-call(s32[3125]{0:T(1024)S(1)} %copy-done, f32[48,128,128]{2,1,0:T(8,128)S(1)} %collective-permute-done.12.refs_1_, ...), custom_call_target="tpu_custom_call", output_to_operand_aliasing={{0}: (2, {}), {1}: (3, {}), {2}: (4, {})} | custom-call | flops 49999998976 | bytes 1 | tf_op jit(solution)/shard_map/products_1/pallas_call | solution.py:262
  52.4 0.0 collective-permute-done.9.refs_4_
  52.4 0.0 collective-permute-done.8.refs_3_
  52.5 0.0 collective-permute-done.16.refs_2_
  52.5 0.0 collective-permute-done.15.refs_1_
  52.5 1.5 %collective-permute-start.14 = (f32[4,128,128]{2,1,0:T(8,128)S(1)}, f32[4,128,128]{2,1,0:T(8,128)S(1)}, u32[]{:S(2)}, u32[]{:S(2)}) collective-permute-start(f32[4,128,128]{2,1,0:T(8,128)S(1)} %slice.39), channel_id=1, source_target_pairs={{0,48},{16,0},{32,16},{48,32},{64,112},{80,64},{96,80},{112,96},{1... | collective-permute-start | bytes 786440 | tf_op jit(solution)/shard_map/ppermute | solution.py:36
  54.0 0.6 collective-permute-start.13
  54.6 0.1 pad_maximum_fusion
  54.7 0.1 collective-permute-start.17
  54.8 3.9 %products_2.1 = (bf16[129,128,256]{2,1,0:T(8,128)(2,1)S(1)}, bf16[64,128,256]{2,1,0:T(8,128)(2,1)S(1)}, f32[32,128,128]{2,1,0:T(8,128)S(1)}) custom-call(s32[3125]{0:T(1024)S(1)} %copy-done, f32[8,128,128]{2,1,0:T(8,128)S(1)} %collective-permute-done.15.refs_1_, ...), custom_call_target="tpu_custom_call", output_to_operand_aliasing={{0}: (5, {}), {1}: (6, {}), {2}: (7, {})} | custom-call | flops 49999998976 | bytes 1 | tf_op jit(solution)/shard_map/products_2/pallas_call | solution.py:262
  58.7 0.0 collective-permute-done.17.refs_1_
  58.7 3.4 %products_3.1 = (bf16[129,128,256]{2,1,0:T(8,128)(2,1)S(1)}, bf16[64,128,256]{2,1,0:T(8,128)(2,1)S(1)}, f32[32,128,128]{2,1,0:T(8,128)S(1)}) custom-call(s32[3125]{0:T(1024)S(1)} %copy-done, f32[16,128,128]{2,1,0:T(8,128)S(1)} %collective-permute-done.17.refs_1_, ...), custom_call_target="tpu_custom_call", output_to_operand_aliasing={{0}: (2, {}), {1}: (3, {}), {2}: (4, {})} | custom-call | flops 49999998976 | bytes 1 | tf_op jit(solution)/shard_map/products_3/pallas_call | solution.py:262
  62.1 0.0 collective-permute-done.14.refs_2_
  62.1 0.1 collective-permute-done.13.refs_1_
  62.2 4.2 %products_4.1 = (bf16[129,128,256]{2,1,0:T(8,128)(2,1)S(1)}, bf16[64,128,256]{2,1,0:T(8,128)(2,1)S(1)}, f32[32,128,128]{2,1,0:T(8,128)S(1)}, f32[32,128,128]{2,1,0:T(8,128)}) custom-call(s32[3125]{0:T(1024)S(1)} %copy-done, f32[4,128,128]{2,1,0:T(8,128)S(1)} %collective-permute-done.13.refs_1_, ...), custom_call_target="tpu_custom_call", output_to_operand_aliasing={{0}: (3, {}), {1}: (4, {}), {2}: (5, {})} | custom-call | flops 49999998976 | bytes 1 | tf_op jit(solution)/shard_map/products_4/pallas_call | solution.py:262
  (19 shorter events, 0.5 us)
Async XLA Ops:
  0.0 15.6 %collective-permute-start.2 = (f32[8,128,128]{2,1,0:T(8,128)}, f32[8,128,128]{2,1,0:T(8,128)S(1)}, u32[]{:S(2)}, u32[]{:S(2)}) collective-permute-start(f32[8,128,128]{2,1,0:T(8,128)} %bitcast.16), channel_id=1, source_target_pairs={{0,6},{1,7},{2,0},{3,1},{4,2},{5,3},{6,4},{7,5},{8,14},{9,15},{10,... | collective-permute-start | bytes 1572872 | tf_op jit(solution)/shard_map/ppermute | solution.py:28
  2.8 14.8 %collective-permute-start.1 = (f32[8,128,128]{2,1,0:T(8,128)}, f32[8,128,128]{2,1,0:T(8,128)S(1)}, u32[]{:S(2)}, u32[]{:S(2)}) collective-permute-start(f32[8,128,128]{2,1,0:T(8,128)} %bitcast.17), channel_id=1, source_target_pairs={{0,2},{1,3},{2,4},{3,5},{4,6},{5,7},{6,0},{7,1},{8,10},{9,11},{10,... | collective-permute-start | bytes 1572872 | tf_op jit(solution)/shard_map/ppermute | solution.py:28
  2.8 14.8 %collective-permute-start = (f32[8,128,128]{2,1,0:T(8,128)}, f32[8,128,128]{2,1,0:T(8,128)S(1)}, u32[]{:S(2)}, u32[]{:S(2)}) collective-permute-start(f32[8,128,128]{2,1,0:T(8,128)} %bitcast.18), channel_id=1, source_target_pairs={{0,8},{1,9},{2,10},{3,11},{4,12},{5,13},{6,14},{7,15},{8,0},{9,1},... | collective-permute-start | bytes 1572872 | tf_op jit(solution)/shard_map/ppermute | solution.py:28
  8.2 16.1 %collective-permute-start.5 = (f32[8,128,128]{2,1,0:T(8,128)}, f32[8,128,128]{2,1,0:T(8,128)S(1)}, u32[]{:S(2)}, u32[]{:S(2)}) collective-permute-start(f32[8,128,128]{2,1,0:T(8,128)} %bitcast.21), channel_id=1, source_target_pairs={{0,48},{16,0},{32,16},{48,32},{64,112},{80,64},{96,80},{112,96},{1... | collective-permute-start | bytes 1572872 | tf_op jit(solution)/shard_map/ppermute | solution.py:36
  12.2 14.2 %collective-permute-start.4 = (f32[8,128,128]{2,1,0:T(8,128)}, f32[8,128,128]{2,1,0:T(8,128)S(1)}, u32[]{:S(2)}, u32[]{:S(2)}) collective-permute-start(f32[8,128,128]{2,1,0:T(8,128)} %bitcast.22), channel_id=1, source_target_pairs={{0,16},{16,32},{32,48},{48,0},{64,80},{80,96},{96,112},{112,64},{1... | collective-permute-start | bytes 1572872 | tf_op jit(solution)/shard_map/ppermute | solution.py:36
  17.7 18.4 %collective-permute-start.3 = (f32[8,128,128]{2,1,0:T(8,128)}, f32[8,128,128]{2,1,0:T(8,128)S(1)}, u32[]{:S(2)}, u32[]{:S(2)}) collective-permute-start(f32[8,128,128]{2,1,0:T(8,128)} %bitcast.23), channel_id=1, source_target_pairs={{0,64},{16,80},{32,96},{48,112},{64,0},{80,16},{96,32},{112,48},{1... | collective-permute-start | bytes 1572872 | tf_op jit(solution)/shard_map/ppermute | solution.py:36
  20.8 17.2 %collective-permute-start.11 = (f32[8,128,128]{2,1,0:T(8,128)S(1)}, f32[8,128,128]{2,1,0:T(8,128)S(1)}, u32[]{:S(2)}, u32[]{:S(2)}) collective-permute-start(f32[8,128,128]{2,1,0:T(8,128)S(1)} %collective-permute-done.refs_2_), channel_id=1, source_target_pairs={{0,6},{1,7},{2,0},{3,1},{4,2},{5,3},{6,4},{7,5},{8,14},{9,15},{10,... | collective-permute-start | bytes 1572872 | tf_op jit(solution)/shard_map/ppermute | solution.py:28
  22.6 15.5 %collective-permute-start.10 = (f32[8,128,128]{2,1,0:T(8,128)S(1)}, f32[8,128,128]{2,1,0:T(8,128)S(1)}, u32[]{:S(2)}, u32[]{:S(2)}) collective-permute-start(f32[8,128,128]{2,1,0:T(8,128)S(1)} %collective-permute-done.refs_2_), channel_id=1, source_target_pairs={{0,2},{1,3},{2,4},{3,5},{4,6},{5,7},{6,0},{7,1},{8,10},{9,11},{10,... | collective-permute-start | bytes 1572872 | tf_op jit(solution)/shard_map/ppermute | solution.py:28
  26.5 6.4 %collective-permute-start.7 = (f32[4,128,128]{2,1,0:T(8,128)S(1)}, f32[4,128,128]{2,1,0:T(8,128)S(1)}, u32[]{:S(2)}, u32[]{:S(2)}) collective-permute-start(f32[4,128,128]{2,1,0:T(8,128)S(1)} %slice.37), channel_id=1, source_target_pairs={{0,48},{16,0},{32,16},{48,32},{64,112},{80,64},{96,80},{112,96},{1... | collective-permute-start | bytes 786440 | tf_op jit(solution)/shard_map/ppermute | solution.py:36
  28.5 7.6 %collective-permute-start.6 = (f32[4,128,128]{2,1,0:T(8,128)S(1)}, f32[4,128,128]{2,1,0:T(8,128)S(1)}, u32[]{:S(2)}, u32[]{:S(2)}) collective-permute-start(f32[4,128,128]{2,1,0:T(8,128)S(1)} %slice.36), channel_id=1, source_target_pairs={{0,16},{16,32},{32,48},{48,0},{64,80},{80,96},{96,112},{112,64},{1... | collective-permute-start | bytes 786440 | tf_op jit(solution)/shard_map/ppermute | solution.py:36
  36.0 16.4 %collective-permute-start.9 = (f32[8,128,128]{2,1,0:T(8,128)S(1)}, f32[8,128,128]{2,1,0:T(8,128)S(1)}, u32[]{:S(2)}, u32[]{:S(2)}) collective-permute-start(f32[8,128,128]{2,1,0:T(8,128)S(1)} %collective-permute-done.3.refs_4_), channel_id=1, source_target_pairs={{0,48},{16,0},{32,16},{48,32},{64,112},{80,64},{96,80},{112,96},{1... | collective-permute-start | bytes 1572872 | tf_op jit(solution)/shard_map/ppermute | solution.py:36
  36.0 16.4 %collective-permute-start.8 = (f32[8,128,128]{2,1,0:T(8,128)S(1)}, f32[8,128,128]{2,1,0:T(8,128)S(1)}, u32[]{:S(2)}, u32[]{:S(2)}) collective-permute-start(f32[8,128,128]{2,1,0:T(8,128)S(1)} %collective-permute-done.3.refs_4_), channel_id=1, source_target_pairs={{0,16},{16,32},{32,48},{48,0},{64,80},{80,96},{96,112},{112,64},{1... | collective-permute-start | bytes 1572872 | tf_op jit(solution)/shard_map/ppermute | solution.py:36
  38.6 3.3 %copy-start.1 = (f32[1,1,8,128,128]{4,3,2,1,0:T(8,128)S(1)}, f32[1,1,8,128,128]{4,3,2,1,0:T(8,128)}, u32[]{:S(2)}) copy-start(f32[1,1,8,128,128]{4,3,2,1,0:T(8,128)} %param.4) | copy-start | bytes 1572868
  38.8 13.7 %collective-permute-start.16 = (f32[8,128,128]{2,1,0:T(8,128)S(1)}, f32[8,128,128]{2,1,0:T(8,128)S(1)}, u32[]{:S(2)}, u32[]{:S(2)}) collective-permute-start(f32[8,128,128]{2,1,0:T(8,128)S(1)} %pad_maximum_fusion.2), channel_id=1, source_target_pairs={{0,6},{1,7},{2,0},{3,1},{4,2},{5,3},{6,4},{7,5},{8,14},{9,15},{10,... | collective-permute-start | bytes 1572872 | tf_op jit(solution)/shard_map/ppermute | solution.py:28
  41.8 0.7 %copy-start = (s32[3125]{0:T(1024)S(1)}, s32[3125]{0:T(1024)}, u32[]{:S(2)}) copy-start(s32[3125]{0:T(1024)} %sort_entries.1.refs_0_) | copy-start | bytes 37504
  41.9 10.7 %collective-permute-start.15 = (f32[8,128,128]{2,1,0:T(8,128)S(1)}, f32[8,128,128]{2,1,0:T(8,128)S(1)}, u32[]{:S(2)}, u32[]{:S(2)}) collective-permute-start(f32[8,128,128]{2,1,0:T(8,128)S(1)} %pad_maximum_fusion.1), channel_id=1, source_target_pairs={{0,2},{1,3},{2,4},{3,5},{4,6},{5,7},{6,0},{7,1},{8,10},{9,11},{10,... | collective-permute-start | bytes 1572872 | tf_op jit(solution)/shard_map/ppermute | solution.py:28
  42.2 5.7 %collective-permute-start.12 = (f32[48,128,128]{2,1,0:T(8,128)S(1)}, f32[48,128,128]{2,1,0:T(8,128)S(1)}, u32[]{:S(2)}, u32[]{:S(2)}) collective-permute-start(f32[48,128,128]{2,1,0:T(8,128)S(1)} %constant_dynamic-update-slice_fusion), channel_id=1, source_target_pairs={{0,1},{1,0},{2,3},{3,2},{4,5},{5,4},{6,7},{7,6},{8,9},{9,8},{10,11... | collective-permute-start | bytes 9437192 | tf_op jit(solution)/shard_map/ppermute | solution.py:28
  52.5 9.6 %collective-permute-start.14 = (f32[4,128,128]{2,1,0:T(8,128)S(1)}, f32[4,128,128]{2,1,0:T(8,128)S(1)}, u32[]{:S(2)}, u32[]{:S(2)}) collective-permute-start(f32[4,128,128]{2,1,0:T(8,128)S(1)} %slice.39), channel_id=1, source_target_pairs={{0,48},{16,0},{32,16},{48,32},{64,112},{80,64},{96,80},{112,96},{1... | collective-permute-start | bytes 786440 | tf_op jit(solution)/shard_map/ppermute | solution.py:36
  54.0 8.2 %collective-permute-start.13 = (f32[4,128,128]{2,1,0:T(8,128)S(1)}, f32[4,128,128]{2,1,0:T(8,128)S(1)}, u32[]{:S(2)}, u32[]{:S(2)}) collective-permute-start(f32[4,128,128]{2,1,0:T(8,128)S(1)} %slice.38), channel_id=1, source_target_pairs={{0,16},{16,32},{32,48},{48,0},{64,80},{80,96},{96,112},{112,64},{1... | collective-permute-start | bytes 786440 | tf_op jit(solution)/shard_map/ppermute | solution.py:36
  54.7 4.0 %collective-permute-start.17 = (f32[16,128,128]{2,1,0:T(8,128)S(1)}, f32[16,128,128]{2,1,0:T(8,128)S(1)}, u32[]{:S(2)}, u32[]{:S(2)}) collective-permute-start(f32[16,128,128]{2,1,0:T(8,128)S(1)} %pad_maximum_fusion), channel_id=1, source_target_pairs={{0,1},{1,0},{2,3},{3,2},{4,5},{5,4},{6,7},{7,6},{8,9},{9,8},{10,11... | collective-permute-start | bytes 3145736 | tf_op jit(solution)/shard_map/ppermute | solution.py:28

commit v3 on v2

--- a/solution.py
+++ b/solution.py
@@ -8,7 +8,7 @@
 from jax.sharding import PartitionSpec as P
 
 CT = 32
-BIG = 32
+GROUPS = (64, 32, 16, 8)
 SMALL = 8
 CLASSES = 5
 LIST = 512 + SMALL
@@ -223,21 +223,17 @@
         for s, m in zip(sums, places):
             c_ref[m] = c_ref[m] + s
 
-    base = stage * LIST
-    count = l_ref[COUNTS + stage]
-    bigs = count // BIG
-    rest = (count - bigs * BIG + SMALL - 1) // SMALL
-
-    def big(g, carry):
-        group(BIG, base + g * BIG)
-        return carry
-
-    def small(g, carry):
-        group(SMALL, base + bigs * BIG + g * SMALL)
-        return carry
-
-    lax.fori_loop(0, bigs, big, 0)
-    lax.fori_loop(0, rest, small, 0)
+    first = stage * LIST
+    left = l_ref[COUNTS + stage]
+    for size in GROUPS:
+        times = jnp.maximum(left + SMALL - 1, 0) // size
+
+        def step(g, carry, size=size, first=first):
+            group(size, first + g * size)
+            return carry
+
+        lax.fori_loop(0, times, step, 0)
+        first, left = first + times * size, left - times * size
     if stage == CLASSES - 1:
         out_hbm, sem = refs[7 + n_in :]
         copy = pltpu.make_async_copy(c_ref, out_hbm, sem)
@@ -280,7 +276,7 @@
     words, b_late = barrier((words, b))
     b03, b01 = move_b(b_late, dz=1), move_b(b_late, dz=-1)
     entries = sort_entries(words)
-    a10, a03, a01, entries, a, b = barrier((a10, a03, a01, entries, a, b))
+    a10, entries, a, b = barrier((a10, entries, a, b))
     b10 = move_b(b, dy=1)
     a13, a11 = move_a(a10, dx=1), move_a(a10, dx=-1)
     state = first_splits(

time: 66.7 us -> 65.5 us (0.982)
  Pallas kernels: 24.8 us -> 18 us
  waiting for transfers between devices: 13.6 us -> 17.4 us
  starting transfers between devices: 23.2 us -> 24.3 us
    pallas_call x5, Pallas kernels: 19.5 us -> 12.7 us  [products(): pl.pallas_call(functools.partial(products_kernel, stage, a_parts, b_parts...]
    ppermute x9, waiting for transfers between devices: 3.9 us -> 6.01 us  [move_a(): return lax.ppermute(value, 'col', pairs)]
    ppermute x9, waiting for transfers between devices: 9.71 us -> 11.4 us  [move_b(): return lax.ppermute(value, 'row', pairs)]
    ppermute x9, starting transfers between devices: 9.71 us -> 10.9 us  [move_a(): return lax.ppermute(value, 'col', pairs)]
  transfers between devices with their start and end apart: 18 -> 18, of which waited for: 6 -> 8; matrix products, arithmetic and copies ran while one was open for 6% -> 7% of each run, Pallas kernels for 31% -> 23%
where the time goes in v3:
time: 65.5 us; the launch traced here: 64.7 us
  starting transfers between devices  24.3 us (37%)
  Pallas kernels  18 us (27%)
  waiting for transfers between devices  17.4 us (27%)
  other arithmetic  2.93 us (4%)
  local copies, waits for them, and re-layouts  1.59 us (2%)
    ppermute x9, starting transfers between devices, move_b(): return lax.ppermute(value, 'row', pairs)  13.4 us
    pallas_call x5, Pallas kernels, products(): pl.pallas_call(functools.partial(products_kernel, stage, a_parts, b_parts...  12.7 us
    ppermute x9, waiting for transfers between devices, move_b(): return lax.ppermute(value, 'row', pairs)  11.4 us
    ppermute x9, starting transfers between devices, move_a(): return lax.ppermute(value, 'col', pairs)  10.9 us
    ppermute x9, waiting for transfers between devices, move_a(): return lax.ppermute(value, 'col', pairs)  6.01 us
    pallas_call x1, Pallas kernels, sort_entries(): pl.pallas_call(sort_kernel, out_shape=jax.ShapeDtypeStruct((COUNTS + CLAS...  3.37 us
    pallas_call x1, Pallas kernels, first_splits(): pl.pallas_call(functools.partial(split_kernel, len(news), a_parts, b_part...  1.39 us
  transfers between devices with their start and end apart: 18, of which 8 were waited for; matrix products, arithmetic and copies ran while one was open for 7% of the time, Pallas kernels for 23%

profile of v3, /device:TPU:0, one launch (start us, length us, event | category | flops | bytes accessed | tf_op | source)
XLA Modules:
  0.0 64.7 jit_solution(12248142223724320030)
XLA Ops:
  0.0 2.8 %collective-permute-start.5 = (f32[8,128,128]{2,1,0:T(8,128)}, f32[8,128,128]{2,1,0:T(8,128)S(1)}, u32[]{:S(2)}, u32[]{:S(2)}) collective-permute-start(f32[8,128,128]{2,1,0:T(8,128)} %bitcast.16), channel_id=1, source_target_pairs={{0,6},{1,7},{2,0},{3,1},{4,2},{5,3},{6,4},{7,5},{8,14},{9,15},{10,... | collective-permute-start | bytes 1572872 | tf_op jit(solution)/shard_map/ppermute | solution.py:28
  2.8 0.0 collective-permute-start.4
  2.8 1.6 %collective-permute-start = (f32[8,128,128]{2,1,0:T(8,128)}, f32[8,128,128]{2,1,0:T(8,128)S(1)}, u32[]{:S(2)}, u32[]{:S(2)}) collective-permute-start(f32[8,128,128]{2,1,0:T(8,128)} %bitcast.18), channel_id=1, source_target_pairs={{0,8},{1,9},{2,10},{3,11},{4,12},{5,13},{6,14},{7,15},{8,0},{9,1},... | collective-permute-start | bytes 1572872 | tf_op jit(solution)/shard_map/ppermute | solution.py:28
  4.4 0.7 %fusion = (pred[16,1,32]{2,0,1:T(8,128)(4,1)S(1)}, pred[16,1,32]{2,0,1:T(8,128)(4,1)S(1)}) fusion(s32[16,3,32]{2,0,1:T(8,128)} %bitcast.25, s32[]{:T(128)S(6)} %axis_index.25, s32[]{:T(128)S(6)} %shift_right_arithmetic.15), kind=kLoop, calls=%fused_computation.16 | loop fusion | flops 4608 | bytes 3080 | tf_op jit(solution)/shard_map/eq | solution.py:51
  5.1 0.7 %fusion.10 = (s32[16,1,32]{2,0,1:T(8,128)S(1)}, s32[16,1,32]{2,0,1:T(8,128)S(1)}, s32[16,1,32]{2,0,1:T(8,128)S(1)}) fusion(s32[16,3,32]{2,0,1:T(8,128)} %bitcast.26, s32[]{:T(128)S(6)} %axis_index.25, s32[]{:T(128)S(6)} %shift_right_arithmetic.15), kind=kLoop, calls=%fused_computation.35 | loop fusion | flops 6144 | bytes 12296 | tf_op jit(solution)/shard_map/slice | solution.py:59
  5.9 0.7 %iota_compare_fusion = pred[16,32]{1,0:T(8,128)(4,1)S(1)} fusion(s32[16]{0:T(128)} %bitcast.28), kind=kLoop, calls=%fused_computation.11 | loop fusion | flops 512 | bytes 576 | tf_op jit(solution)/shard_map/lt | solution.py:63
  6.6 0.1 broadcast_in_dim.35
  6.7 0.1 broadcast_in_dim.36
  6.8 0.1 lt.23
  6.9 0.1 reshape.129
  7.0 0.1 reshape.132
  7.1 0.1 broadcast_in_dim.37
  7.1 0.1 broadcast_in_dim.38
  7.2 0.1 add.54
  7.3 0.1 add.55
  7.4 0.1 squeeze.16
  7.4 0.1 reshape.135
  7.5 0.1 shift_left.24
  7.6 0.6 shift-left_or_fusion.w_ref
  8.2 4.0 %collective-permute-start.3 = (f32[8,128,128]{2,1,0:T(8,128)}, f32[8,128,128]{2,1,0:T(8,128)S(1)}, u32[]{:S(2)}, u32[]{:S(2)}) collective-permute-start(f32[8,128,128]{2,1,0:T(8,128)} %bitcast.21), channel_id=1, source_target_pairs={{0,48},{16,0},{32,16},{48,32},{64,112},{80,64},{96,80},{112,96},{1... | collective-permute-start | bytes 1572872 | tf_op jit(solution)/shard_map/ppermute | solution.py:36
  12.2 0.0 collective-permute-start.2
  12.2 3.4 %sort_entries.1.refs_0_ = s32[3125]{0:T(1024)} custom-call(s32[512]{0:T(512)} %shift-left_or_fusion.w_ref, s32[1,512]{1,0:T(1,128)} %bitcast.27), custom_call_target="tpu_custom_call" | custom-call | bytes 16000000 | tf_op jit(solution)/shard_map/sort_entries/pallas_call | solution.py:118
  15.6 0.8 %collective-permute-done.refs_2_ = f32[8,128,128]{2,1,0:T(8,128)S(1)} collective-permute-done((f32[8,128,128]{2,1,0:T(8,128)}, f32[8,128,128]{2,1,0:T(8,128)S(1)}, u32[]{:S(2)}, u32[]{:S(2)}) %collective-permute-start) | collective-permute-done | bytes 524320 | tf_op jit(solution)/shard_map/ppermute | solution.py:28
  16.4 3.2 %collective-permute-start.1 = (f32[8,128,128]{2,1,0:T(8,128)}, f32[8,128,128]{2,1,0:T(8,128)S(1)}, u32[]{:S(2)}, u32[]{:S(2)}) collective-permute-start(f32[8,128,128]{2,1,0:T(8,128)} %bitcast.23), channel_id=1, source_target_pairs={{0,64},{16,80},{32,96},{48,112},{64,0},{80,16},{96,32},{112,48},{1... | collective-permute-start | bytes 1572872 | tf_op jit(solution)/shard_map/ppermute | solution.py:36
  19.6 0.0 collective-permute-done.5.refs_4_
  19.6 3.0 %collective-permute-start.11 = (f32[8,128,128]{2,1,0:T(8,128)S(1)}, f32[8,128,128]{2,1,0:T(8,128)S(1)}, u32[]{:S(2)}, u32[]{:S(2)}) collective-permute-start(f32[8,128,128]{2,1,0:T(8,128)S(1)} %collective-permute-done.refs_2_), channel_id=1, source_target_pairs={{0,6},{1,7},{2,0},{3,1},{4,2},{5,3},{6,4},{7,5},{8,14},{9,15},{10,... | collective-permute-start | bytes 1572872 | tf_op jit(solution)/shard_map/ppermute | solution.py:28
  22.6 0.0 collective-permute-done.4.refs_3_
  22.6 0.0 collective-permute-start.10
  22.6 1.4 %first_splits.1 = (bf16[129,128,256]{2,1,0:T(8,128)(2,1)S(1)}, bf16[64,128,256]{2,1,0:T(8,128)(2,1)S(1)}, f32[32,128,128]{2,1,0:T(8,128)S(1)}) custom-call(f32[8,128,128]{2,1,0:T(8,128)} %bitcast.19, f32[8,128,128]{2,1,0:T(8,128)} %bitcast.24, f32[8,128,128]{2,1,0:T(8,128)S(1)} %collective-permute-done.refs_2_, ...), custom_call_target="tpu_custom_call" | custom-call | bytes 4000000 | tf_op jit(solution)/shard_map/first_splits/pallas_call | solution.py:168
  24.0 0.0 collective-permute-done.3.refs_3_
  24.0 2.5 %collective-permute-done.2.refs_2_ = f32[8,128,128]{2,1,0:T(8,128)S(1)} collective-permute-done((f32[8,128,128]{2,1,0:T(8,128)}, f32[8,128,128]{2,1,0:T(8,128)S(1)}, u32[]{:S(2)}, u32[]{:S(2)}) %collective-permute-start.2) | collective-permute-done | bytes 524320 | tf_op jit(solution)/shard_map/ppermute | solution.py:36
  26.5 1.7 %collective-permute-start.7 = (f32[4,128,128]{2,1,0:T(8,128)S(1)}, f32[4,128,128]{2,1,0:T(8,128)S(1)}, u32[]{:S(2)}, u32[]{:S(2)}) collective-permute-start(f32[4,128,128]{2,1,0:T(8,128)S(1)} %slice.37), channel_id=1, source_target_pairs={{0,48},{16,0},{32,16},{48,32},{64,112},{80,64},{96,80},{112,96},{1... | collective-permute-start | bytes 786440 | tf_op jit(solution)/shard_map/ppermute | solution.py:36
  28.2 0.4 collective-permute-start.6
  28.6 4.3 %collective-permute-done.7.refs_6_ = f32[4,128,128]{2,1,0:T(8,128)S(1)} collective-permute-done((f32[4,128,128]{2,1,0:T(8,128)S(1)}, f32[4,128,128]{2,1,0:T(8,128)S(1)}, u32[]{:S(2)}, u32[]{:S(2)}) %collective-permute-start.7) | collective-permute-done | bytes 262176 | tf_op jit(solution)/shard_map/ppermute | solution.py:36
  33.0 2.8 %collective-permute-done.6.refs_5_ = f32[4,128,128]{2,1,0:T(8,128)S(1)} collective-permute-done((f32[4,128,128]{2,1,0:T(8,128)S(1)}, f32[4,128,128]{2,1,0:T(8,128)S(1)}, u32[]{:S(2)}, u32[]{:S(2)}) %collective-permute-start.6) | collective-permute-done | bytes 262176 | tf_op jit(solution)/shard_map/ppermute | solution.py:36
  35.8 0.0 collective-permute-done.1.refs_4_
  35.8 0.0 collective-permute-start.9
  35.8 2.0 %collective-permute-start.8 = (f32[8,128,128]{2,1,0:T(8,128)S(1)}, f32[8,128,128]{2,1,0:T(8,128)S(1)}, u32[]{:S(2)}, u32[]{:S(2)}) collective-permute-start(f32[8,128,128]{2,1,0:T(8,128)S(1)} %collective-permute-done.1.refs_4_), channel_id=1, source_target_pairs={{0,16},{16,32},{32,48},{48,0},{64,80},{80,96},{96,112},{112,64},{1... | collective-permute-start | bytes 1572872 | tf_op jit(solution)/shard_map/ppermute | solution.py:36
  37.8 0.0 collective-permute-done.11.refs_1_
  37.8 0.0 collective-permute-done.10.refs_0_
  37.8 0.5 more_splits.1
  38.3 0.0 copy-start.1
  38.5 3.3 %collective-permute-start.16 = (f32[8,128,128]{2,1,0:T(8,128)S(1)}, f32[8,128,128]{2,1,0:T(8,128)S(1)}, u32[]{:S(2)}, u32[]{:S(2)}) collective-permute-start(f32[8,128,128]{2,1,0:T(8,128)S(1)} %pad_maximum_fusion.2), channel_id=1, source_target_pairs={{0,6},{1,7},{2,0},{3,1},{4,2},{5,3},{6,4},{7,5},{8,14},{9,15},{10,... | collective-permute-start | bytes 1572872 | tf_op jit(solution)/shard_map/ppermute | solution.py:28
  41.9 0.0 copy-start
  41.9 0.1 collective-permute-start.15
  42.2 0.1 collective-permute-start.12
  42.3 0.3 copy-done
  42.6 2.3 %products_0.1 = (bf16[129,128,256]{2,1,0:T(8,128)(2,1)S(1)}, bf16[64,128,256]{2,1,0:T(8,128)(2,1)S(1)}, f32[32,128,128]{2,1,0:T(8,128)S(1)}) custom-call(s32[3125]{0:T(1024)S(1)} %copy-done, bf16[129,128,256]{2,1,0:T(8,128)(2,1)S(1)} %get-tuple-element.80.refs_1_, ...), custom_call_target="tpu_custom_call", output_to_operand_aliasing={{0}: (1, {}), {1}: (2, {}), {2}: (3, {})} | custom-call | flops 49999998976 | bytes 1 | tf_op jit(solution)/shard_map/products_0/pallas_call | solution.py:258
  44.9 3.1 %collective-permute-done.12.refs_1_ = f32[48,128,128]{2,1,0:T(8,128)S(1)} collective-permute-done((f32[48,128,128]{2,1,0:T(8,128)S(1)}, f32[48,128,128]{2,1,0:T(8,128)S(1)}, u32[]{:S(2)}, u32[]{:S(2)}) %collective-permute-start.12) | collective-permute-done | bytes 3145760 | tf_op jit(solution)/shard_map/ppermute | solution.py:28
  48.0 2.8 %products_1.1 = (bf16[129,128,256]{2,1,0:T(8,128)(2,1)S(1)}, bf16[64,128,256]{2,1,0:T(8,128)(2,1)S(1)}, f32[32,128,128]{2,1,0:T(8,128)S(1)}) custom-call(s32[3125]{0:T(1024)S(1)} %copy-done, f32[48,128,128]{2,1,0:T(8,128)S(1)} %collective-permute-done.12.refs_1_, ...), custom_call_target="tpu_custom_call", output_to_operand_aliasing={{0}: (2, {}), {1}: (3, {}), {2}: (4, {})} | custom-call | flops 49999998976 | bytes 1 | tf_op jit(solution)/shard_map/products_1/pallas_call | solution.py:258
  50.8 0.0 collective-permute-done.9.refs_4_
  50.8 0.0 collective-permute-done.8.refs_3_
  50.8 0.0 collective-permute-done.16.refs_2_
  50.8 1.7 %collective-permute-done.15.refs_1_ = f32[8,128,128]{2,1,0:T(8,128)S(1)} collective-permute-done((f32[8,128,128]{2,1,0:T(8,128)S(1)}, f32[8,128,128]{2,1,0:T(8,128)S(1)}, u32[]{:S(2)}, u32[]{:S(2)}) %collective-permute-start.15) | collective-permute-done | bytes 524320 | tf_op jit(solution)/shard_map/ppermute | solution.py:28
  52.5 1.5 %collective-permute-start.14 = (f32[4,128,128]{2,1,0:T(8,128)S(1)}, f32[4,128,128]{2,1,0:T(8,128)S(1)}, u32[]{:S(2)}, u32[]{:S(2)}) collective-permute-start(f32[4,128,128]{2,1,0:T(8,128)S(1)} %slice.39), channel_id=1, source_target_pairs={{0,48},{16,0},{32,16},{48,32},{64,112},{80,64},{96,80},{112,96},{1... | collective-permute-start | bytes 786440 | tf_op jit(solution)/shard_map/ppermute | solution.py:36
  54.0 0.5 collective-permute-start.13
  54.5 0.1 pad_maximum_fusion
  54.6 0.1 collective-permute-start.17
  54.7 2.2 %products_2.1 = (bf16[129,128,256]{2,1,0:T(8,128)(2,1)S(1)}, bf16[64,128,256]{2,1,0:T(8,128)(2,1)S(1)}, f32[32,128,128]{2,1,0:T(8,128)S(1)}) custom-call(s32[3125]{0:T(1024)S(1)} %copy-done, f32[8,128,128]{2,1,0:T(8,128)S(1)} %collective-permute-done.15.refs_1_, ...), custom_call_target="tpu_custom_call", output_to_operand_aliasing={{0}: (5, {}), {1}: (6, {}), {2}: (7, {})} | custom-call | flops 49999998976 | bytes 1 | tf_op jit(solution)/shard_map/products_2/pallas_call | solution.py:258
  56.9 0.4 collective-permute-done.17.refs_1_
  57.3 2.5 %products_3.1 = (bf16[129,128,256]{2,1,0:T(8,128)(2,1)S(1)}, bf16[64,128,256]{2,1,0:T(8,128)(2,1)S(1)}, f32[32,128,128]{2,1,0:T(8,128)S(1)}) custom-call(s32[3125]{0:T(1024)S(1)} %copy-done, f32[16,128,128]{2,1,0:T(8,128)S(1)} %collective-permute-done.17.refs_1_, ...), custom_call_target="tpu_custom_call", output_to_operand_aliasing={{0}: (2, {}), {1}: (3, {}), {2}: (4, {})} | custom-call | flops 49999998976 | bytes 1 | tf_op jit(solution)/shard_map/products_3/pallas_call | solution.py:258
  59.8 0.0 collective-permute-done.14.refs_2_
  59.8 1.7 %collective-permute-done.13.refs_1_ = f32[4,128,128]{2,1,0:T(8,128)S(1)} collective-permute-done((f32[4,128,128]{2,1,0:T(8,128)S(1)}, f32[4,128,128]{2,1,0:T(8,128)S(1)}, u32[]{:S(2)}, u32[]{:S(2)}) %collective-permute-start.13) | collective-permute-done | bytes 262176 | tf_op jit(solution)/shard_map/ppermute | solution.py:36
  61.6 2.9 %products_4.1 = (bf16[129,128,256]{2,1,0:T(8,128)(2,1)S(1)}, bf16[64,128,256]{2,1,0:T(8,128)(2,1)S(1)}, f32[32,128,128]{2,1,0:T(8,128)S(1)}, f32[32,128,128]{2,1,0:T(8,128)}) custom-call(s32[3125]{0:T(1024)S(1)} %copy-done, f32[4,128,128]{2,1,0:T(8,128)S(1)} %collective-permute-done.13.refs_1_, ...), custom_call_target="tpu_custom_call", output_to_operand_aliasing={{0}: (3, {}), {1}: (4, {}), {2}: (5, {})} | custom-call | flops 49999998976 | bytes 1 | tf_op jit(solution)/shard_map/products_4/pallas_call | solution.py:258
  (19 shorter events, 0.5 us)
Async XLA Ops:
  0.0 19.6 %collective-permute-start.5 = (f32[8,128,128]{2,1,0:T(8,128)}, f32[8,128,128]{2,1,0:T(8,128)S(1)}, u32[]{:S(2)}, u32[]{:S(2)}) collective-permute-start(f32[8,128,128]{2,1,0:T(8,128)} %bitcast.16), channel_id=1, source_target_pairs={{0,6},{1,7},{2,0},{3,1},{4,2},{5,3},{6,4},{7,5},{8,14},{9,15},{10,... | collective-permute-start | bytes 1572872 | tf_op jit(solution)/shard_map/ppermute | solution.py:28
  2.8 19.8 %collective-permute-start.4 = (f32[8,128,128]{2,1,0:T(8,128)}, f32[8,128,128]{2,1,0:T(8,128)S(1)}, u32[]{:S(2)}, u32[]{:S(2)}) collective-permute-start(f32[8,128,128]{2,1,0:T(8,128)} %bitcast.17), channel_id=1, source_target_pairs={{0,2},{1,3},{2,4},{3,5},{4,6},{5,7},{6,0},{7,1},{8,10},{9,11},{10,... | collective-permute-start | bytes 1572872 | tf_op jit(solution)/shard_map/ppermute | solution.py:28
  2.8 13.6 %collective-permute-start = (f32[8,128,128]{2,1,0:T(8,128)}, f32[8,128,128]{2,1,0:T(8,128)S(1)}, u32[]{:S(2)}, u32[]{:S(2)}) collective-permute-start(f32[8,128,128]{2,1,0:T(8,128)} %bitcast.18), channel_id=1, source_target_pairs={{0,8},{1,9},{2,10},{3,11},{4,12},{5,13},{6,14},{7,15},{8,0},{9,1},... | collective-permute-start | bytes 1572872 | tf_op jit(solution)/shard_map/ppermute | solution.py:28
  8.2 15.8 %collective-permute-start.3 = (f32[8,128,128]{2,1,0:T(8,128)}, f32[8,128,128]{2,1,0:T(8,128)S(1)}, u32[]{:S(2)}, u32[]{:S(2)}) collective-permute-start(f32[8,128,128]{2,1,0:T(8,128)} %bitcast.21), channel_id=1, source_target_pairs={{0,48},{16,0},{32,16},{48,32},{64,112},{80,64},{96,80},{112,96},{1... | collective-permute-start | bytes 1572872 | tf_op jit(solution)/shard_map/ppermute | solution.py:36
  12.2 14.2 %collective-permute-start.2 = (f32[8,128,128]{2,1,0:T(8,128)}, f32[8,128,128]{2,1,0:T(8,128)S(1)}, u32[]{:S(2)}, u32[]{:S(2)}) collective-permute-start(f32[8,128,128]{2,1,0:T(8,128)} %bitcast.22), channel_id=1, source_target_pairs={{0,16},{16,32},{32,48},{48,0},{64,80},{80,96},{96,112},{112,64},{1... | collective-permute-start | bytes 1572872 | tf_op jit(solution)/shard_map/ppermute | solution.py:36
  16.4 19.3 %collective-permute-start.1 = (f32[8,128,128]{2,1,0:T(8,128)}, f32[8,128,128]{2,1,0:T(8,128)S(1)}, u32[]{:S(2)}, u32[]{:S(2)}) collective-permute-start(f32[8,128,128]{2,1,0:T(8,128)} %bitcast.23), channel_id=1, source_target_pairs={{0,64},{16,80},{32,96},{48,112},{64,0},{80,16},{96,32},{112,48},{1... | collective-permute-start | bytes 1572872 | tf_op jit(solution)/shard_map/ppermute | solution.py:36
  19.6 18.2 %collective-permute-start.11 = (f32[8,128,128]{2,1,0:T(8,128)S(1)}, f32[8,128,128]{2,1,0:T(8,128)S(1)}, u32[]{:S(2)}, u32[]{:S(2)}) collective-permute-start(f32[8,128,128]{2,1,0:T(8,128)S(1)} %collective-permute-done.refs_2_), channel_id=1, source_target_pairs={{0,6},{1,7},{2,0},{3,1},{4,2},{5,3},{6,4},{7,5},{8,14},{9,15},{10,... | collective-permute-start | bytes 1572872 | tf_op jit(solution)/shard_map/ppermute | solution.py:28
  22.6 15.2 %collective-permute-start.10 = (f32[8,128,128]{2,1,0:T(8,128)S(1)}, f32[8,128,128]{2,1,0:T(8,128)S(1)}, u32[]{:S(2)}, u32[]{:S(2)}) collective-permute-start(f32[8,128,128]{2,1,0:T(8,128)S(1)} %collective-permute-done.refs_2_), channel_id=1, source_target_pairs={{0,2},{1,3},{2,4},{3,5},{4,6},{5,7},{6,0},{7,1},{8,10},{9,11},{10,... | collective-permute-start | bytes 1572872 | tf_op jit(solution)/shard_map/ppermute | solution.py:28
  26.5 6.4 %collective-permute-start.7 = (f32[4,128,128]{2,1,0:T(8,128)S(1)}, f32[4,128,128]{2,1,0:T(8,128)S(1)}, u32[]{:S(2)}, u32[]{:S(2)}) collective-permute-start(f32[4,128,128]{2,1,0:T(8,128)S(1)} %slice.37), channel_id=1, source_target_pairs={{0,48},{16,0},{32,16},{48,32},{64,112},{80,64},{96,80},{112,96},{1... | collective-permute-start | bytes 786440 | tf_op jit(solution)/shard_map/ppermute | solution.py:36
  28.2 7.6 %collective-permute-start.6 = (f32[4,128,128]{2,1,0:T(8,128)S(1)}, f32[4,128,128]{2,1,0:T(8,128)S(1)}, u32[]{:S(2)}, u32[]{:S(2)}) collective-permute-start(f32[4,128,128]{2,1,0:T(8,128)S(1)} %slice.36), channel_id=1, source_target_pairs={{0,16},{16,32},{32,48},{48,0},{64,80},{80,96},{96,112},{112,64},{1... | collective-permute-start | bytes 786440 | tf_op jit(solution)/shard_map/ppermute | solution.py:36
  35.8 15.0 %collective-permute-start.9 = (f32[8,128,128]{2,1,0:T(8,128)S(1)}, f32[8,128,128]{2,1,0:T(8,128)S(1)}, u32[]{:S(2)}, u32[]{:S(2)}) collective-permute-start(f32[8,128,128]{2,1,0:T(8,128)S(1)} %collective-permute-done.1.refs_4_), channel_id=1, source_target_pairs={{0,48},{16,0},{32,16},{48,32},{64,112},{80,64},{96,80},{112,96},{1... | collective-permute-start | bytes 1572872 | tf_op jit(solution)/shard_map/ppermute | solution.py:36
  35.8 15.0 %collective-permute-start.8 = (f32[8,128,128]{2,1,0:T(8,128)S(1)}, f32[8,128,128]{2,1,0:T(8,128)S(1)}, u32[]{:S(2)}, u32[]{:S(2)}) collective-permute-start(f32[8,128,128]{2,1,0:T(8,128)S(1)} %collective-permute-done.1.refs_4_), channel_id=1, source_target_pairs={{0,16},{16,32},{32,48},{48,0},{64,80},{80,96},{96,112},{112,64},{1... | collective-permute-start | bytes 1572872 | tf_op jit(solution)/shard_map/ppermute | solution.py:36
  38.3 3.6 %copy-start.1 = (f32[1,1,8,128,128]{4,3,2,1,0:T(8,128)S(1)}, f32[1,1,8,128,128]{4,3,2,1,0:T(8,128)}, u32[]{:S(2)}) copy-start(f32[1,1,8,128,128]{4,3,2,1,0:T(8,128)} %param.4) | copy-start | bytes 1572868
  38.5 12.3 %collective-permute-start.16 = (f32[8,128,128]{2,1,0:T(8,128)S(1)}, f32[8,128,128]{2,1,0:T(8,128)S(1)}, u32[]{:S(2)}, u32[]{:S(2)}) collective-permute-start(f32[8,128,128]{2,1,0:T(8,128)S(1)} %pad_maximum_fusion.2), channel_id=1, source_target_pairs={{0,6},{1,7},{2,0},{3,1},{4,2},{5,3},{6,4},{7,5},{8,14},{9,15},{10,... | collective-permute-start | bytes 1572872 | tf_op jit(solution)/shard_map/ppermute | solution.py:28
  41.9 0.7 %copy-start = (s32[3125]{0:T(1024)S(1)}, s32[3125]{0:T(1024)}, u32[]{:S(2)}) copy-start(s32[3125]{0:T(1024)} %sort_entries.1.refs_0_) | copy-start | bytes 37504
  41.9 10.6 %collective-permute-start.15 = (f32[8,128,128]{2,1,0:T(8,128)S(1)}, f32[8,128,128]{2,1,0:T(8,128)S(1)}, u32[]{:S(2)}, u32[]{:S(2)}) collective-permute-start(f32[8,128,128]{2,1,0:T(8,128)S(1)} %pad_maximum_fusion.1), channel_id=1, source_target_pairs={{0,2},{1,3},{2,4},{3,5},{4,6},{5,7},{6,0},{7,1},{8,10},{9,11},{10,... | collective-permute-start | bytes 1572872 | tf_op jit(solution)/shard_map/ppermute | solution.py:28
  42.2 5.7 %collective-permute-start.12 = (f32[48,128,128]{2,1,0:T(8,128)S(1)}, f32[48,128,128]{2,1,0:T(8,128)S(1)}, u32[]{:S(2)}, u32[]{:S(2)}) collective-permute-start(f32[48,128,128]{2,1,0:T(8,128)S(1)} %constant_dynamic-update-slice_fusion), channel_id=1, source_target_pairs={{0,1},{1,0},{2,3},{3,2},{4,5},{5,4},{6,7},{7,6},{8,9},{9,8},{10,11... | collective-permute-start | bytes 9437192 | tf_op jit(solution)/shard_map/ppermute | solution.py:28
  52.5 7.3 %collective-permute-start.14 = (f32[4,128,128]{2,1,0:T(8,128)S(1)}, f32[4,128,128]{2,1,0:T(8,128)S(1)}, u32[]{:S(2)}, u32[]{:S(2)}) collective-permute-start(f32[4,128,128]{2,1,0:T(8,128)S(1)} %slice.39), channel_id=1, source_target_pairs={{0,48},{16,0},{32,16},{48,32},{64,112},{80,64},{96,80},{112,96},{1... | collective-permute-start | bytes 786440 | tf_op jit(solution)/shard_map/ppermute | solution.py:36
  54.0 7.6 %collective-permute-start.13 = (f32[4,128,128]{2,1,0:T(8,128)S(1)}, f32[4,128,128]{2,1,0:T(8,128)S(1)}, u32[]{:S(2)}, u32[]{:S(2)}) collective-permute-start(f32[4,128,128]{2,1,0:T(8,128)S(1)} %slice.38), channel_id=1, source_target_pairs={{0,16},{16,32},{32,48},{48,0},{64,80},{80,96},{96,112},{112,64},{1... | collective-permute-start | bytes 786440 | tf_op jit(solution)/shard_map/ppermute | solution.py:36
  54.6 2.7 %collective-permute-start.17 = (f32[16,128,128]{2,1,0:T(8,128)S(1)}, f32[16,128,128]{2,1,0:T(8,128)S(1)}, u32[]{:S(2)}, u32[]{:S(2)}) collective-permute-start(f32[16,128,128]{2,1,0:T(8,128)S(1)} %pad_maximum_fusion), channel_id=1, source_target_pairs={{0,1},{1,0},{2,3},{3,2},{4,5},{5,4},{6,7},{7,6},{8,9},{9,8},{10,11... | collective-permute-start | bytes 3145736 | tf_op jit(solution)/shard_map/ppermute | solution.py:28

commit v4 on v3

--- a/solution.py
+++ b/solution.py
@@ -271,9 +271,10 @@
 def body(a_tiles, b_tiles, pair_lists, stack_counts):
     barrier = lax.optimization_barrier
     a, b = a_tiles[0, 0], b_tiles[0, 0]
-    a10, a03, a01 = move_a(a, dy=1), move_a(a, dx=1), move_a(a, dx=-1)
+    a10 = move_a(a, dy=1)
     words = packed_entries(pair_lists[0, 0], stack_counts[0, 0])
-    words, b_late = barrier((words, b))
+    words, a_late, b_late = barrier((words, a, b))
+    a03, a01 = move_a(a_late, dx=1), move_a(a_late, dx=-1)
     b03, b01 = move_b(b_late, dz=1), move_b(b_late, dz=-1)
     entries = sort_entries(words)
     a10, entries, a, b = barrier((a10, entries, a, b))

time: 65.5 us -> 66.3 us (1.012)
  transfers between devices with their start and end apart: 18 -> 18, of which waited for: 8 -> 8; matrix products, arithmetic and copies ran while one was open for 7% -> 6% of each run, Pallas kernels for 23% -> 23%
where the time goes in v4:
time: 66.3 us; the launch traced here: 65.7 us
  starting transfers between devices  24.7 us (37%)
  Pallas kernels  18 us (27%)
  waiting for transfers between devices  18 us (27%)
  other arithmetic  2.93 us (4%)
  local copies, waits for them, and re-layouts  1.59 us (2%)
    ppermute x9, starting transfers between devices, move_b(): return lax.ppermute(value, 'row', pairs)  13.2 us
    pallas_call x5, Pallas kernels, products(): pl.pallas_call(functools.partial(products_kernel, stage, a_parts, b_parts...  12.7 us
    ppermute x9, starting transfers between devices, move_a(): return lax.ppermute(value, 'col', pairs)  11.6 us
    ppermute x9, waiting for transfers between devices, move_b(): return lax.ppermute(value, 'row', pairs)  11.4 us
    ppermute x9, waiting for transfers between devices, move_a(): return lax.ppermute(value, 'col', pairs)  6.57 us
    pallas_call x1, Pallas kernels, sort_entries(): pl.pallas_call(sort_kernel, out_shape=jax.ShapeDtypeStruct((COUNTS + CLAS...  3.37 us
    pallas_call x1, Pallas kernels, first_splits(): pl.pallas_call(functools.partial(split_kernel, len(news), a_parts, b_part...  1.39 us
  transfers between devices with their start and end apart: 18, of which 8 were waited for; matrix products, arithmetic and copies ran while one was open for 6% of the time, Pallas kernels for 23%

profile of v4, /device:TPU:0, one launch (start us, length us, event | category | flops | bytes accessed | tf_op | source)
XLA Modules:
  0.0 65.7 jit_solution(5807586179829661791)
XLA Ops:
  0.0 1.7 %collective-permute-start = (f32[8,128,128]{2,1,0:T(8,128)}, f32[8,128,128]{2,1,0:T(8,128)S(1)}, u32[]{:S(2)}, u32[]{:S(2)}) collective-permute-start(f32[8,128,128]{2,1,0:T(8,128)} %bitcast.16), channel_id=1, source_target_pairs={{0,8},{1,9},{2,10},{3,11},{4,12},{5,13},{6,14},{7,15},{8,0},{9,1},... | collective-permute-start | bytes 1572872 | tf_op jit(solution)/shard_map/ppermute | solution.py:28
  1.7 0.7 %fusion = (pred[16,1,32]{2,0,1:T(8,128)(4,1)S(1)}, pred[16,1,32]{2,0,1:T(8,128)(4,1)S(1)}) fusion(s32[16,3,32]{2,0,1:T(8,128)} %bitcast.25, s32[]{:T(128)S(6)} %axis_index.25, s32[]{:T(128)S(6)} %shift_right_arithmetic.15), kind=kLoop, calls=%fused_computation.16 | loop fusion | flops 4608 | bytes 3080 | tf_op jit(solution)/shard_map/eq | solution.py:51
  2.4 0.7 %fusion.10 = (s32[16,1,32]{2,0,1:T(8,128)S(1)}, s32[16,1,32]{2,0,1:T(8,128)S(1)}, s32[16,1,32]{2,0,1:T(8,128)S(1)}) fusion(s32[16,3,32]{2,0,1:T(8,128)} %bitcast.26, s32[]{:T(128)S(6)} %axis_index.25, s32[]{:T(128)S(6)} %shift_right_arithmetic.15), kind=kLoop, calls=%fused_computation.35 | loop fusion | flops 6144 | bytes 12296 | tf_op jit(solution)/shard_map/slice | solution.py:59
  3.1 0.1 broadcast_in_dim.35
  3.2 0.1 broadcast_in_dim.36
  3.3 0.7 %iota_compare_fusion = pred[16,32]{1,0:T(8,128)(4,1)S(1)} fusion(s32[16]{0:T(128)} %bitcast.28), kind=kLoop, calls=%fused_computation.11 | loop fusion | flops 512 | bytes 576 | tf_op jit(solution)/shard_map/lt | solution.py:63
  4.0 0.1 lt.23
  4.1 0.1 reshape.129
  4.2 0.1 reshape.132
  4.3 0.1 broadcast_in_dim.37
  4.4 0.1 broadcast_in_dim.38
  4.5 0.1 add.54
  4.5 0.1 add.55
  4.6 0.1 squeeze.16
  4.7 0.1 reshape.135
  4.8 0.1 shift_left.24
  4.8 0.6 shift-left_or_fusion.w_ref
  5.4 2.8 %collective-permute-start.5 = (f32[8,128,128]{2,1,0:T(8,128)}, f32[8,128,128]{2,1,0:T(8,128)S(1)}, u32[]{:S(2)}, u32[]{:S(2)}) collective-permute-start(f32[8,128,128]{2,1,0:T(8,128)} %bitcast.17), channel_id=1, source_target_pairs={{0,6},{1,7},{2,0},{3,1},{4,2},{5,3},{6,4},{7,5},{8,14},{9,15},{10,... | collective-permute-start | bytes 1572872 | tf_op jit(solution)/shard_map/ppermute | solution.py:28
  8.2 0.0 collective-permute-start.4
  8.2 4.0 %collective-permute-start.3 = (f32[8,128,128]{2,1,0:T(8,128)}, f32[8,128,128]{2,1,0:T(8,128)S(1)}, u32[]{:S(2)}, u32[]{:S(2)}) collective-permute-start(f32[8,128,128]{2,1,0:T(8,128)} %bitcast.21), channel_id=1, source_target_pairs={{0,48},{16,0},{32,16},{48,32},{64,112},{80,64},{96,80},{112,96},{1... | collective-permute-start | bytes 1572872 | tf_op jit(solution)/shard_map/ppermute | solution.py:36
  12.2 0.0 collective-permute-start.2
  12.2 3.4 %sort_entries.1.refs_0_ = s32[3125]{0:T(1024)} custom-call(s32[512]{0:T(512)} %shift-left_or_fusion.w_ref, s32[1,512]{1,0:T(1,128)} %bitcast.27), custom_call_target="tpu_custom_call" | custom-call | bytes 16000000 | tf_op jit(solution)/shard_map/sort_entries/pallas_call | solution.py:118
  15.6 0.0 collective-permute-done.refs_2_
  15.6 3.0 %collective-permute-start.1 = (f32[8,128,128]{2,1,0:T(8,128)}, f32[8,128,128]{2,1,0:T(8,128)S(1)}, u32[]{:S(2)}, u32[]{:S(2)}) collective-permute-start(f32[8,128,128]{2,1,0:T(8,128)} %bitcast.23), channel_id=1, source_target_pairs={{0,64},{16,80},{32,96},{48,112},{64,0},{80,16},{96,32},{112,48},{1... | collective-permute-start | bytes 1572872 | tf_op jit(solution)/shard_map/ppermute | solution.py:36
  18.6 0.8 %collective-permute-done.5.refs_4_ = f32[8,128,128]{2,1,0:T(8,128)S(1)} collective-permute-done((f32[8,128,128]{2,1,0:T(8,128)}, f32[8,128,128]{2,1,0:T(8,128)S(1)}, u32[]{:S(2)}, u32[]{:S(2)}) %collective-permute-start.5) | collective-permute-done | bytes 524320 | tf_op jit(solution)/shard_map/ppermute | solution.py:28
  19.4 3.6 %collective-permute-start.11 = (f32[8,128,128]{2,1,0:T(8,128)S(1)}, f32[8,128,128]{2,1,0:T(8,128)S(1)}, u32[]{:S(2)}, u32[]{:S(2)}) collective-permute-start(f32[8,128,128]{2,1,0:T(8,128)S(1)} %collective-permute-done.refs_2_), channel_id=1, source_target_pairs={{0,6},{1,7},{2,0},{3,1},{4,2},{5,3},{6,4},{7,5},{8,14},{9,15},{10,... | collective-permute-start | bytes 1572872 | tf_op jit(solution)/shard_map/ppermute | solution.py:28
  23.0 0.0 collective-permute-done.4.refs_3_
  23.0 0.0 collective-permute-start.10
  23.0 1.4 %first_splits.1 = (bf16[129,128,256]{2,1,0:T(8,128)(2,1)S(1)}, bf16[64,128,256]{2,1,0:T(8,128)(2,1)S(1)}, f32[32,128,128]{2,1,0:T(8,128)S(1)}) custom-call(f32[8,128,128]{2,1,0:T(8,128)} %bitcast.19, f32[8,128,128]{2,1,0:T(8,128)} %bitcast.24, f32[8,128,128]{2,1,0:T(8,128)S(1)} %collective-permute-done.refs_2_, ...), custom_call_target="tpu_custom_call" | custom-call | bytes 4000000 | tf_op jit(solution)/shard_map/first_splits/pallas_call | solution.py:168
  24.4 0.0 collective-permute-done.3.refs_3_
  24.4 2.1 %collective-permute-done.2.refs_2_ = f32[8,128,128]{2,1,0:T(8,128)S(1)} collective-permute-done((f32[8,128,128]{2,1,0:T(8,128)}, f32[8,128,128]{2,1,0:T(8,128)S(1)}, u32[]{:S(2)}, u32[]{:S(2)}) %collective-permute-start.2) | collective-permute-done | bytes 524320 | tf_op jit(solution)/shard_map/ppermute | solution.py:36
  26.5 2.1 %collective-permute-start.7 = (f32[4,128,128]{2,1,0:T(8,128)S(1)}, f32[4,128,128]{2,1,0:T(8,128)S(1)}, u32[]{:S(2)}, u32[]{:S(2)}) collective-permute-start(f32[4,128,128]{2,1,0:T(8,128)S(1)} %slice.37), channel_id=1, source_target_pairs={{0,48},{16,0},{32,16},{48,32},{64,112},{80,64},{96,80},{112,96},{1... | collective-permute-start | bytes 786440 | tf_op jit(solution)/shard_map/ppermute | solution.py:36
  28.6 0.0 collective-permute-start.6
  28.6 4.3 %collective-permute-done.7.refs_6_ = f32[4,128,128]{2,1,0:T(8,128)S(1)} collective-permute-done((f32[4,128,128]{2,1,0:T(8,128)S(1)}, f32[4,128,128]{2,1,0:T(8,128)S(1)}, u32[]{:S(2)}, u32[]{:S(2)}) %collective-permute-start.7) | collective-permute-done | bytes 262176 | tf_op jit(solution)/shard_map/ppermute | solution.py:36
  33.0 3.2 %collective-permute-done.6.refs_5_ = f32[4,128,128]{2,1,0:T(8,128)S(1)} collective-permute-done((f32[4,128,128]{2,1,0:T(8,128)S(1)}, f32[4,128,128]{2,1,0:T(8,128)S(1)}, u32[]{:S(2)}, u32[]{:S(2)}) %collective-permute-start.6) | collective-permute-done | bytes 262176 | tf_op jit(solution)/shard_map/ppermute | solution.py:36
  36.2 0.0 collective-permute-done.1.refs_4_
  36.2 0.2 collective-permute-start.9
  36.4 1.8 %collective-permute-start.8 = (f32[8,128,128]{2,1,0:T(8,128)S(1)}, f32[8,128,128]{2,1,0:T(8,128)S(1)}, u32[]{:S(2)}, u32[]{:S(2)}) collective-permute-start(f32[8,128,128]{2,1,0:T(8,128)S(1)} %collective-permute-done.1.refs_4_), channel_id=1, source_target_pairs={{0,16},{16,32},{32,48},{48,0},{64,80},{80,96},{96,112},{112,64},{1... | collective-permute-start | bytes 1572872 | tf_op jit(solution)/shard_map/ppermute | solution.py:36
  38.2 0.0 collective-permute-done.11.refs_1_
  38.2 0.0 collective-permute-done.10.refs_0_
  38.2 0.5 more_splits.1
  38.8 0.0 copy-start.1
  38.9 3.3 %collective-permute-start.16 = (f32[8,128,128]{2,1,0:T(8,128)S(1)}, f32[8,128,128]{2,1,0:T(8,128)S(1)}, u32[]{:S(2)}, u32[]{:S(2)}) collective-permute-start(f32[8,128,128]{2,1,0:T(8,128)S(1)} %pad_maximum_fusion.2), channel_id=1, source_target_pairs={{0,6},{1,7},{2,0},{3,1},{4,2},{5,3},{6,4},{7,5},{8,14},{9,15},{10,... | collective-permute-start | bytes 1572872 | tf_op jit(solution)/shard_map/ppermute | solution.py:28
  42.3 0.0 copy-start
  42.3 0.1 collective-permute-start.15
  42.6 0.1 collective-permute-start.12
  42.7 0.3 copy-done
  43.0 2.3 %products_0.1 = (bf16[129,128,256]{2,1,0:T(8,128)(2,1)S(1)}, bf16[64,128,256]{2,1,0:T(8,128)(2,1)S(1)}, f32[32,128,128]{2,1,0:T(8,128)S(1)}) custom-call(s32[3125]{0:T(1024)S(1)} %copy-done, bf16[129,128,256]{2,1,0:T(8,128)(2,1)S(1)} %get-tuple-element.82.refs_1_, ...), custom_call_target="tpu_custom_call", output_to_operand_aliasing={{0}: (1, {}), {1}: (2, {}), {2}: (3, {})} | custom-call | flops 49999998976 | bytes 1 | tf_op jit(solution)/shard_map/products_0/pallas_call | solution.py:258
  45.3 3.1 %collective-permute-done.12.refs_1_ = f32[48,128,128]{2,1,0:T(8,128)S(1)} collective-permute-done((f32[48,128,128]{2,1,0:T(8,128)S(1)}, f32[48,128,128]{2,1,0:T(8,128)S(1)}, u32[]{:S(2)}, u32[]{:S(2)}) %collective-permute-start.12) | collective-permute-done | bytes 3145760 | tf_op jit(solution)/shard_map/ppermute | solution.py:28
  48.4 2.8 %products_1.1 = (bf16[129,128,256]{2,1,0:T(8,128)(2,1)S(1)}, bf16[64,128,256]{2,1,0:T(8,128)(2,1)S(1)}, f32[32,128,128]{2,1,0:T(8,128)S(1)}) custom-call(s32[3125]{0:T(1024)S(1)} %copy-done, f32[48,128,128]{2,1,0:T(8,128)S(1)} %collective-permute-done.12.refs_1_, ...), custom_call_target="tpu_custom_call", output_to_operand_aliasing={{0}: (2, {}), {1}: (3, {}), {2}: (4, {})} | custom-call | flops 49999998976 | bytes 1 | tf_op jit(solution)/shard_map/products_1/pallas_call | solution.py:258
  51.2 0.0 collective-permute-done.9.refs_4_
  51.2 0.0 collective-permute-done.8.refs_3_
  51.3 0.0 collective-permute-done.16.refs_2_
  51.3 2.2 %collective-permute-done.15.refs_1_ = f32[8,128,128]{2,1,0:T(8,128)S(1)} collective-permute-done((f32[8,128,128]{2,1,0:T(8,128)S(1)}, f32[8,128,128]{2,1,0:T(8,128)S(1)}, u32[]{:S(2)}, u32[]{:S(2)}) %collective-permute-start.15) | collective-permute-done | bytes 524320 | tf_op jit(solution)/shard_map/ppermute | solution.py:28
  53.5 1.5 %collective-permute-start.14 = (f32[4,128,128]{2,1,0:T(8,128)S(1)}, f32[4,128,128]{2,1,0:T(8,128)S(1)}, u32[]{:S(2)}, u32[]{:S(2)}) collective-permute-start(f32[4,128,128]{2,1,0:T(8,128)S(1)} %slice.39), channel_id=1, source_target_pairs={{0,48},{16,0},{32,16},{48,32},{64,112},{80,64},{96,80},{112,96},{1... | collective-permute-start | bytes 786440 | tf_op jit(solution)/shard_map/ppermute | solution.py:36
  55.0 0.5 collective-permute-start.13
  55.5 0.1 pad_maximum_fusion
  55.6 0.1 collective-permute-start.17
  55.7 2.2 %products_2.1 = (bf16[129,128,256]{2,1,0:T(8,128)(2,1)S(1)}, bf16[64,128,256]{2,1,0:T(8,128)(2,1)S(1)}, f32[32,128,128]{2,1,0:T(8,128)S(1)}) custom-call(s32[3125]{0:T(1024)S(1)} %copy-done, f32[8,128,128]{2,1,0:T(8,128)S(1)} %collective-permute-done.15.refs_1_, ...), custom_call_target="tpu_custom_call", output_to_operand_aliasing={{0}: (5, {}), {1}: (6, {}), {2}: (7, {})} | custom-call | flops 49999998976 | bytes 1 | tf_op jit(solution)/shard_map/products_2/pallas_call | solution.py:258
  57.9 0.4 collective-permute-done.17.refs_1_
  58.3 2.5 %products_3.1 = (bf16[129,128,256]{2,1,0:T(8,128)(2,1)S(1)}, bf16[64,128,256]{2,1,0:T(8,128)(2,1)S(1)}, f32[32,128,128]{2,1,0:T(8,128)S(1)}) custom-call(s32[3125]{0:T(1024)S(1)} %copy-done, f32[16,128,128]{2,1,0:T(8,128)S(1)} %collective-permute-done.17.refs_1_, ...), custom_call_target="tpu_custom_call", output_to_operand_aliasing={{0}: (2, {}), {1}: (3, {}), {2}: (4, {})} | custom-call | flops 49999998976 | bytes 1 | tf_op jit(solution)/shard_map/products_3/pallas_call | solution.py:258
  60.8 0.0 collective-permute-done.14.refs_2_
  60.8 1.8 %collective-permute-done.13.refs_1_ = f32[4,128,128]{2,1,0:T(8,128)S(1)} collective-permute-done((f32[4,128,128]{2,1,0:T(8,128)S(1)}, f32[4,128,128]{2,1,0:T(8,128)S(1)}, u32[]{:S(2)}, u32[]{:S(2)}) %collective-permute-start.13) | collective-permute-done | bytes 262176 | tf_op jit(solution)/shard_map/ppermute | solution.py:36
  62.6 3.0 %products_4.1 = (bf16[129,128,256]{2,1,0:T(8,128)(2,1)S(1)}, bf16[64,128,256]{2,1,0:T(8,128)(2,1)S(1)}, f32[32,128,128]{2,1,0:T(8,128)S(1)}, f32[32,128,128]{2,1,0:T(8,128)}) custom-call(s32[3125]{0:T(1024)S(1)} %copy-done, f32[4,128,128]{2,1,0:T(8,128)S(1)} %collective-permute-done.13.refs_1_, ...), custom_call_target="tpu_custom_call", output_to_operand_aliasing={{0}: (3, {}), {1}: (4, {}), {2}: (5, {})} | custom-call | flops 49999998976 | bytes 1 | tf_op jit(solution)/shard_map/products_4/pallas_call | solution.py:258
  (19 shorter events, 0.5 us)
Async XLA Ops:
  0.0 15.6 %collective-permute-start = (f32[8,128,128]{2,1,0:T(8,128)}, f32[8,128,128]{2,1,0:T(8,128)S(1)}, u32[]{:S(2)}, u32[]{:S(2)}) collective-permute-start(f32[8,128,128]{2,1,0:T(8,128)} %bitcast.16), channel_id=1, source_target_pairs={{0,8},{1,9},{2,10},{3,11},{4,12},{5,13},{6,14},{7,15},{8,0},{9,1},... | collective-permute-start | bytes 1572872 | tf_op jit(solution)/shard_map/ppermute | solution.py:28
  5.4 14.0 %collective-permute-start.5 = (f32[8,128,128]{2,1,0:T(8,128)}, f32[8,128,128]{2,1,0:T(8,128)S(1)}, u32[]{:S(2)}, u32[]{:S(2)}) collective-permute-start(f32[8,128,128]{2,1,0:T(8,128)} %bitcast.17), channel_id=1, source_target_pairs={{0,6},{1,7},{2,0},{3,1},{4,2},{5,3},{6,4},{7,5},{8,14},{9,15},{10,... | collective-permute-start | bytes 1572872 | tf_op jit(solution)/shard_map/ppermute | solution.py:28
  8.2 14.8 %collective-permute-start.4 = (f32[8,128,128]{2,1,0:T(8,128)}, f32[8,128,128]{2,1,0:T(8,128)S(1)}, u32[]{:S(2)}, u32[]{:S(2)}) collective-permute-start(f32[8,128,128]{2,1,0:T(8,128)} %bitcast.18), channel_id=1, source_target_pairs={{0,2},{1,3},{2,4},{3,5},{4,6},{5,7},{6,0},{7,1},{8,10},{9,11},{10,... | collective-permute-start | bytes 1572872 | tf_op jit(solution)/shard_map/ppermute | solution.py:28
  8.2 16.2 %collective-permute-start.3 = (f32[8,128,128]{2,1,0:T(8,128)}, f32[8,128,128]{2,1,0:T(8,128)S(1)}, u32[]{:S(2)}, u32[]{:S(2)}) collective-permute-start(f32[8,128,128]{2,1,0:T(8,128)} %bitcast.21), channel_id=1, source_target_pairs={{0,48},{16,0},{32,16},{48,32},{64,112},{80,64},{96,80},{112,96},{1... | collective-permute-start | bytes 1572872 | tf_op jit(solution)/shard_map/ppermute | solution.py:36
  12.2 14.2 %collective-permute-start.2 = (f32[8,128,128]{2,1,0:T(8,128)}, f32[8,128,128]{2,1,0:T(8,128)S(1)}, u32[]{:S(2)}, u32[]{:S(2)}) collective-permute-start(f32[8,128,128]{2,1,0:T(8,128)} %bitcast.22), channel_id=1, source_target_pairs={{0,16},{16,32},{32,48},{48,0},{64,80},{80,96},{96,112},{112,64},{1... | collective-permute-start | bytes 1572872 | tf_op jit(solution)/shard_map/ppermute | solution.py:36
  15.6 20.5 %collective-permute-start.1 = (f32[8,128,128]{2,1,0:T(8,128)}, f32[8,128,128]{2,1,0:T(8,128)S(1)}, u32[]{:S(2)}, u32[]{:S(2)}) collective-permute-start(f32[8,128,128]{2,1,0:T(8,128)} %bitcast.23), channel_id=1, source_target_pairs={{0,64},{16,80},{32,96},{48,112},{64,0},{80,16},{96,32},{112,48},{1... | collective-permute-start | bytes 1572872 | tf_op jit(solution)/shard_map/ppermute | solution.py:36
  19.4 18.8 %collective-permute-start.11 = (f32[8,128,128]{2,1,0:T(8,128)S(1)}, f32[8,128,128]{2,1,0:T(8,128)S(1)}, u32[]{:S(2)}, u32[]{:S(2)}) collective-permute-start(f32[8,128,128]{2,1,0:T(8,128)S(1)} %collective-permute-done.refs_2_), channel_id=1, source_target_pairs={{0,6},{1,7},{2,0},{3,1},{4,2},{5,3},{6,4},{7,5},{8,14},{9,15},{10,... | collective-permute-start | bytes 1572872 | tf_op jit(solution)/shard_map/ppermute | solution.py:28
  23.0 15.2 %collective-permute-start.10 = (f32[8,128,128]{2,1,0:T(8,128)S(1)}, f32[8,128,128]{2,1,0:T(8,128)S(1)}, u32[]{:S(2)}, u32[]{:S(2)}) collective-permute-start(f32[8,128,128]{2,1,0:T(8,128)S(1)} %collective-permute-done.refs_2_), channel_id=1, source_target_pairs={{0,2},{1,3},{2,4},{3,5},{4,6},{5,7},{6,0},{7,1},{8,10},{9,11},{10,... | collective-permute-start | bytes 1572872 | tf_op jit(solution)/shard_map/ppermute | solution.py:28
  26.5 6.4 %collective-permute-start.7 = (f32[4,128,128]{2,1,0:T(8,128)S(1)}, f32[4,128,128]{2,1,0:T(8,128)S(1)}, u32[]{:S(2)}, u32[]{:S(2)}) collective-permute-start(f32[4,128,128]{2,1,0:T(8,128)S(1)} %slice.37), channel_id=1, source_target_pairs={{0,48},{16,0},{32,16},{48,32},{64,112},{80,64},{96,80},{112,96},{1... | collective-permute-start | bytes 786440 | tf_op jit(solution)/shard_map/ppermute | solution.py:36
  28.6 7.6 %collective-permute-start.6 = (f32[4,128,128]{2,1,0:T(8,128)S(1)}, f32[4,128,128]{2,1,0:T(8,128)S(1)}, u32[]{:S(2)}, u32[]{:S(2)}) collective-permute-start(f32[4,128,128]{2,1,0:T(8,128)S(1)} %slice.36), channel_id=1, source_target_pairs={{0,16},{16,32},{32,48},{48,0},{64,80},{80,96},{96,112},{112,64},{1... | collective-permute-start | bytes 786440 | tf_op jit(solution)/shard_map/ppermute | solution.py:36
  36.2 15.0 %collective-permute-start.9 = (f32[8,128,128]{2,1,0:T(8,128)S(1)}, f32[8,128,128]{2,1,0:T(8,128)S(1)}, u32[]{:S(2)}, u32[]{:S(2)}) collective-permute-start(f32[8,128,128]{2,1,0:T(8,128)S(1)} %collective-permute-done.1.refs_4_), channel_id=1, source_target_pairs={{0,48},{16,0},{32,16},{48,32},{64,112},{80,64},{96,80},{112,96},{1... | collective-permute-start | bytes 1572872 | tf_op jit(solution)/shard_map/ppermute | solution.py:36
  36.4 14.8 %collective-permute-start.8 = (f32[8,128,128]{2,1,0:T(8,128)S(1)}, f32[8,128,128]{2,1,0:T(8,128)S(1)}, u32[]{:S(2)}, u32[]{:S(2)}) collective-permute-start(f32[8,128,128]{2,1,0:T(8,128)S(1)} %collective-permute-done.1.refs_4_), channel_id=1, source_target_pairs={{0,16},{16,32},{32,48},{48,0},{64,80},{80,96},{96,112},{112,64},{1... | collective-permute-start | bytes 1572872 | tf_op jit(solution)/shard_map/ppermute | solution.py:36
  38.8 3.6 %copy-start.1 = (f32[1,1,8,128,128]{4,3,2,1,0:T(8,128)S(1)}, f32[1,1,8,128,128]{4,3,2,1,0:T(8,128)}, u32[]{:S(2)}) copy-start(f32[1,1,8,128,128]{4,3,2,1,0:T(8,128)} %param.4) | copy-start | bytes 1572868
  38.9 12.3 %collective-permute-start.16 = (f32[8,128,128]{2,1,0:T(8,128)S(1)}, f32[8,128,128]{2,1,0:T(8,128)S(1)}, u32[]{:S(2)}, u32[]{:S(2)}) collective-permute-start(f32[8,128,128]{2,1,0:T(8,128)S(1)} %pad_maximum_fusion.2), channel_id=1, source_target_pairs={{0,6},{1,7},{2,0},{3,1},{4,2},{5,3},{6,4},{7,5},{8,14},{9,15},{10,... | collective-permute-start | bytes 1572872 | tf_op jit(solution)/shard_map/ppermute | solution.py:28
  42.3 0.7 %copy-start = (s32[3125]{0:T(1024)S(1)}, s32[3125]{0:T(1024)}, u32[]{:S(2)}) copy-start(s32[3125]{0:T(1024)} %sort_entries.1.refs_0_) | copy-start | bytes 37504
  42.3 11.2 %collective-permute-start.15 = (f32[8,128,128]{2,1,0:T(8,128)S(1)}, f32[8,128,128]{2,1,0:T(8,128)S(1)}, u32[]{:S(2)}, u32[]{:S(2)}) collective-permute-start(f32[8,128,128]{2,1,0:T(8,128)S(1)} %pad_maximum_fusion.1), channel_id=1, source_target_pairs={{0,2},{1,3},{2,4},{3,5},{4,6},{5,7},{6,0},{7,1},{8,10},{9,11},{10,... | collective-permute-start | bytes 1572872 | tf_op jit(solution)/shard_map/ppermute | solution.py:28
  42.6 5.7 %collective-permute-start.12 = (f32[48,128,128]{2,1,0:T(8,128)S(1)}, f32[48,128,128]{2,1,0:T(8,128)S(1)}, u32[]{:S(2)}, u32[]{:S(2)}) collective-permute-start(f32[48,128,128]{2,1,0:T(8,128)S(1)} %constant_dynamic-update-slice_fusion), channel_id=1, source_target_pairs={{0,1},{1,0},{2,3},{3,2},{4,5},{5,4},{6,7},{7,6},{8,9},{9,8},{10,11... | collective-permute-start | bytes 9437192 | tf_op jit(solution)/shard_map/ppermute | solution.py:28
  53.5 7.3 %collective-permute-start.14 = (f32[4,128,128]{2,1,0:T(8,128)S(1)}, f32[4,128,128]{2,1,0:T(8,128)S(1)}, u32[]{:S(2)}, u32[]{:S(2)}) collective-permute-start(f32[4,128,128]{2,1,0:T(8,128)S(1)} %slice.39), channel_id=1, source_target_pairs={{0,48},{16,0},{32,16},{48,32},{64,112},{80,64},{96,80},{112,96},{1... | collective-permute-start | bytes 786440 | tf_op jit(solution)/shard_map/ppermute | solution.py:36
  55.0 7.6 %collective-permute-start.13 = (f32[4,128,128]{2,1,0:T(8,128)S(1)}, f32[4,128,128]{2,1,0:T(8,128)S(1)}, u32[]{:S(2)}, u32[]{:S(2)}) collective-permute-start(f32[4,128,128]{2,1,0:T(8,128)S(1)} %slice.38), channel_id=1, source_target_pairs={{0,16},{16,32},{32,48},{48,0},{64,80},{80,96},{96,112},{112,64},{1... | collective-permute-start | bytes 786440 | tf_op jit(solution)/shard_map/ppermute | solution.py:36
  55.6 2.7 %collective-permute-start.17 = (f32[16,128,128]{2,1,0:T(8,128)S(1)}, f32[16,128,128]{2,1,0:T(8,128)S(1)}, u32[]{:S(2)}, u32[]{:S(2)}) collective-permute-start(f32[16,128,128]{2,1,0:T(8,128)S(1)} %pad_maximum_fusion), channel_id=1, source_target_pairs={{0,1},{1,0},{2,3},{3,2},{4,5},{5,4},{6,7},{7,6},{8,9},{9,8},{10,11... | collective-permute-start | bytes 3145736 | tf_op jit(solution)/shard_map/ppermute | solution.py:28
